TPU v7x, 128 devices: a whole 4x4x4 slice. The times are simulated.
128 devices in a mesh: ctx: 32 (over x_lo, y, z), fft: 4 (over x_hi, core).
Axes of the slice: x: 4 (x_hi: 2, x_lo: 2; x = x_hi * 2 + x_lo), y: 4, z: 4, core: 2. Of those that a mesh axis runs over, the one named last changes fastest.
Arguments:
- qkv: bfloat16 [16384, 3, 4096], P('ctx', None, 'fft'), may hold values from -6 to 6
- short_w: bfloat16 [3, 3, 4096], P(None, None, 'fft'), may hold values from -3.5 to 3.5
- skip: float32 [4096], P('fft'), may hold values from -4 to 4
- long_h: float32 [4, 32, 2, 16384], P(None, 'ctx'), may hold values from -1 to 1
Outputs:
- hyena_out: bfloat16 [16384, 4096], P('ctx', 'fft')
All inputs are finite; a program needn't handle non-finite values.
Results may differ from a plain program's by a relative error of at most 0.0075.
Values may be sent and summed in bfloat16 or wider, within the bound.
No kernel may reach another device: no remote copies, remote signals or barrier semaphores. Data moves between devices by JAX's collectives and lax.ppermute only.
A program may use at most 128 MiB of HBM per device.

v0:
```python
import math

import jax
import jax.numpy as jnp
from jax import lax
from jax.sharding import PartitionSpec as P

GROUP = 16


def shifted(value, axis, steps):
    count = lax.axis_size(axis)
    first, last = (max(0, -steps), min(count, count - steps))
    return lax.ppermute(value, axis, [(source, source + steps) for source in range(first, last)])


def valid_depthwise(signal, kernel):
    taps = kernel.shape[0]
    rows = signal.shape[0] - (taps - 1)
    wide_signal = signal.astype(jnp.float32)
    kernel_wide = kernel.astype(jnp.float32)
    total = kernel_wide[0][None, :] * wide_signal[taps - 1 : taps - 1 + rows]
    for offset in range(1, taps):
        total = (
            total
            + kernel_wide[offset][None, :]
            * wide_signal[taps - 1 - offset : taps - 1 - offset + rows]
        )
    return total


def split_length(total, half_rows):
    second = 1
    for candidate in range(1, total + 1):
        if candidate * candidate > total:
            break
        if half_rows % candidate == 0:
            second = candidate
    return (total // second, second)


def dft_tables(first, second):
    total = first * second
    index_one = jnp.arange(first, dtype=jnp.int32)
    index_two = jnp.arange(second, dtype=jnp.int32)
    angle_one = (
        2.0
        * math.pi
        / first
        * (index_one[:, None] * index_one[None, :] % first).astype(jnp.float32)
    )
    angle_two = (
        2.0
        * math.pi
        / second
        * (index_two[:, None] * index_two[None, :] % second).astype(jnp.float32)
    )
    angle_mid = (
        2.0
        * math.pi
        / total
        * (index_one[:, None] * index_two[None, :] % total).astype(jnp.float32)
    )
    return (
        jnp.cos(angle_one),
        jnp.sin(angle_one),
        jnp.cos(angle_two),
        jnp.sin(angle_two),
        jnp.cos(angle_mid),
        jnp.sin(angle_mid),
    )


def contract(form, table, data):
    return jnp.einsum(form, table, data, precision=lax.Precision.HIGHEST)


def spectrum(signal, tables, lead):
    cos_one, sin_one, cos_two, sin_two, cos_mid, sin_mid = tables
    if lead:
        used_rows = signal.shape[1]
        first_form, second_form = ("kn,cnm->ckm", "lm,ckm->ckl")
        turn_cos, turn_sin = (cos_mid[None], sin_mid[None])
    else:
        used_rows = signal.shape[0]
        first_form, second_form = ("kn,nmc->kmc", "lm,kmc->klc")
        turn_cos, turn_sin = (cos_mid[:, :, None], sin_mid[:, :, None])
    part_re = contract(first_form, cos_one[:, :used_rows], signal)
    part_im = -contract(first_form, sin_one[:, :used_rows], signal)
    turned_re = part_re * turn_cos + part_im * turn_sin
    turned_im = part_im * turn_cos - part_re * turn_sin
    out_re = contract(second_form, cos_two, turned_re) + contract(second_form, sin_two, turned_im)
    out_im = contract(second_form, cos_two, turned_im) - contract(second_form, sin_two, turned_re)
    return (out_re, out_im)


def signal_half(spec_re, spec_im, tables):
    cos_one, sin_one, cos_two, sin_two, cos_mid, sin_mid = tables
    first = cos_one.shape[0]
    total = first * cos_two.shape[0]
    first_form, last_form = ("lm,klc->kmc", "nk,kmc->nmc")
    turn_cos, turn_sin = (cos_mid[:, :, None], sin_mid[:, :, None])
    mixed_re = contract(first_form, cos_two, spec_re) - contract(first_form, sin_two, spec_im)
    mixed_im = contract(first_form, cos_two, spec_im) + contract(first_form, sin_two, spec_re)
    turned_re = mixed_re * turn_cos - mixed_im * turn_sin
    turned_im = mixed_im * turn_cos + mixed_re * turn_sin
    half_rows = first // 2
    rows_cos = cos_one[half_rows : half_rows + half_rows]
    rows_sin = sin_one[half_rows : half_rows + half_rows]
    return (
        contract(last_form, rows_cos, turned_re) - contract(last_form, rows_sin, turned_im)
    ) / total


def local(qkv, short_w, skip, long_h):
    tok_rows = qkv.shape[0]
    channels = qkv.shape[2]
    k_short = short_w.shape[0]
    kernel_short = short_w.reshape(k_short, 3 * channels)
    short_rim = shifted(qkv[tok_rows - (k_short - 1) :], "ctx", 1)
    extended = jnp.concatenate([short_rim, qkv], axis=0).reshape(
        tok_rows + k_short - 1, 3 * channels
    )
    feat = valid_depthwise(extended, kernel_short)
    query = feat[:, :channels]
    gated = (feat[:, channels : 2 * channels] * feat[:, 2 * channels :]).astype(jnp.bfloat16)
    columns = lax.all_to_all(
        lax.all_to_all(gated, "ctx", split_axis=1, concat_axis=0, tiled=True),
        "fft",
        split_axis=0,
        concat_axis=1,
        tiled=True,
    )
    quarter_rows = columns.shape[0]
    long_ch = columns.shape[1]
    first, second = split_length(2 * quarter_rows, quarter_rows)
    tables = dft_tables(first, second)
    own_fft = lax.axis_index("fft")
    taps = long_h.reshape(-1, long_h.shape[-1])
    padded_taps = jnp.concatenate(
        [jnp.zeros((taps.shape[0], quarter_rows), jnp.float32), taps], axis=1
    )

    def filter_spectrum(lag_block):
        segment = lax.dynamic_slice_in_dim(
            padded_taps, lag_block * quarter_rows, 2 * quarter_rows, 1
        )
        seg_re, seg_im = spectrum(segment.reshape(taps.shape[0], first, second), tables, True)
        seg_re = jnp.repeat(jnp.moveaxis(seg_re, 0, -1), GROUP, axis=-1)
        seg_im = jnp.repeat(jnp.moveaxis(seg_im, 0, -1), GROUP, axis=-1)
        return (seg_re, seg_im)

    def block_spectrum(block_rows):
        return spectrum(
            block_rows.astype(jnp.float32).reshape(first // 2, second, long_ch), tables, False
        )

    def add_block(carry, block_rows, source_start):
        lag_block = own_fft - source_start // quarter_rows

        def compute_sum(state):
            data_re, data_im = block_spectrum(block_rows)
            filt_re, filt_im = filter_spectrum(lag_block)
            return (
                state[0] + data_re * filt_re - data_im * filt_im,
                state[1] + data_re * filt_im + data_im * filt_re,
            )

        def keep_sum(state):
            return state

        return lax.cond(lag_block >= 0, compute_sum, keep_sum, carry)

    zeros_spec = jnp.zeros((first, second, long_ch), jnp.float32)
    carry = (zeros_spec, zeros_spec)
    piece = jax.tree.map(lambda part: lax.all_gather(part, "fft", axis=0, tiled=True), columns)
    start = jnp.int32(0)
    count = piece.shape[0]
    if count >= quarter_rows:
        for symbol_ordinal in range(count // quarter_rows):
            carry = add_block(
                carry,
                piece[symbol_ordinal * quarter_rows : (symbol_ordinal + 1) * quarter_rows],
                start + symbol_ordinal * quarter_rows,
            )
    else:
        offset = start % quarter_rows
        buffer = lax.dynamic_update_slice_in_dim(
            jnp.zeros((quarter_rows, long_ch), piece.dtype), piece, offset, 0
        )
        carry = add_block(carry, buffer, start - offset)
    total_re, total_im = carry
    long_rows = signal_half(total_re, total_im, tables).reshape(quarter_rows, long_ch)
    back = lax.all_to_all(
        lax.all_to_all(
            long_rows.astype(jnp.bfloat16), "fft", split_axis=1, concat_axis=0, tiled=True
        ),
        "ctx",
        split_axis=0,
        concat_axis=1,
        tiled=True,
    )
    inner = back.astype(jnp.float32) + skip[None, :] * gated.astype(jnp.float32)
    return (query * inner).astype(jnp.bfloat16)


def solution(mesh):
    in_specs = (P("ctx", None, "fft"), P(None, None, "fft"), P("fft"), P(None, "ctx", None, None))
    out_specs = P("ctx", "fft")
    return jax.shard_map(local, mesh=mesh, in_specs=in_specs, out_specs=out_specs, check_vma=False)
```

profile of v0, /device:TPU:6, one launch (start us, length us, event | category | flops | bytes accessed | tf_op | source)
XLA Modules:
  0.0 503.4 jit_solution(6000404525314179390)
XLA Ops:
  7.4 3.8 collective-permute-start
  11.9 4.7 copy.195
  18.1 3.6 maximum_convert_fusion
  21.8 6.8 %fusion.206 = (f32[512,3,1024]{0,2,1:T(8,128)S(1)}, f32[512,3,1024]{0,2,1:T(8,128)}, f32[512,3,1024]{0,2,1:T(8,128)}) fusion(f32[514,3,1024]{0,2,1:T(8,128)S(1)} %maximum_convert_fusion), kind=kLoop, calls=%fused_computation.267 | loop fusion | bytes 37748736 | tf_op jit(solution)/shard_map/slice | solution.py:22
  28.6 5.6 %fusion.146 = f32[512,3072]{0,1:T(8,128)S(1)} fusion(f32[512,3,1024]{0,2,1:T(8,128)} %get-tuple-element.585, f32[512,3,1024]{0,2,1:T(8,128)} %get-tuple-element.586, f32[512,3,1024]{0,2,1:T(8,128)S(1)} %get-tuple-element.584, f32[3072]{0:T(1024)S(1)} %mul.1169, f32[3072]{0:T(1024)S(1)} %mul.1166, f32[3072]{0:T(1024)S(1)} %mul.1163), kind=kLoop, calls=%fused_computation.191 | loop fusion | flops 7864320 | bytes 25202688 | tf_op jit(solution)/shard_map/add | solution.py:25
  34.2 2.6 copy-done
  37.2 24.1 %all_to_all.61 = bf16[512,32,32]{0,2,1:T(8,128)(2,1)S(1)} all-to-all(bf16[512,32,32]{0,2,1:T(8,128)(2,1)S(1)} %bitcast.356), channel_id=1, replica_groups=mesh['ctx'=32,'fft'=4] {'ctx'}, dimensions={1} | all-to-all | bytes 2097152 | tf_op jit(solution)/shard_map/all_to_all | solution.py:128
  63.3 17.7 %all_to_all.62 = bf16[4,4096,32]{1,2,0:T(8,128)(2,1)} all-to-all(bf16[4,4096,32]{1,2,0:T(8,128)(2,1)S(1)} %copy.197), channel_id=1, replica_groups=mesh['ctx'=32,'fft'=4] {'fft'}, dimensions={0} | all-to-all | bytes 2097152 | tf_op jit(solution)/shard_map/all_to_all | solution.py:127
  82.3 33.7 %all-gather.2.cloned.1.call-done = bf16[16384,128]{0,1:T(8,128)(2,1)} async-done(((bf16[4096,128]{0,1:T(8,128)(2,1)}), bf16[16384,128]{0,1:T(8,128)(2,1)}) %all-gather.2.cloned.1.call-update) | async-done | bytes 4194320 | tf_op jit(solution)/shard_map/all_gather | solution.py:176
  116.0 3.6 fusion.207
  119.6 65.8 %conditional.4 = (f32[128,64,128]{2,1,0:T(8,128)}, f32[128,64,128]{2,1,0:T(8,128)}) conditional(s32[]{:T(128)} %convert_element_type.245, () %tuple.31, (f32[128,128]{1,0:T(8,128)S(1)}, bf16[4096,128]{0,1:T(8,128)(2,1)}, f32[128,64]{0,1:T(8,128)S(1)}, f32[128,64]{0,1:T(8,128)S(1)}, f32[128,128]{1,0:T(8,128)S(1)}, /*index=5*/f32[128,64]{0,1:T(8,128)S(1)}, ...), branch_computations={%region_0.1_spmd, %region_1.2_spmd} | conditional | flops 5251203072 | bytes 146735232 | solution.py:172
  125.1 5.4 %copy.149 = f32[128,64,128]{2,1,0:T(8,128)} copy(f32[128,64,128]{0,2,1:T(8,128)} %bitcast.340) | data formatting | bytes 8388608 | tf_op jit(solution)/shard_map/cond/branch_1_fun/reshape | solution.py:150
  133.8 5.4 %copy.145 = f32[128,64,128]{2,1,0:T(8,128)} copy(f32[128,64,128]{0,2,1:T(8,128)} %bitcast.341) | data formatting | bytes 8388608 | tf_op jit(solution)/shard_map/cond/branch_1_fun/reshape | solution.py:149
  140.9 4.0 fusion.19
  145.0 9.0 %multiply_add_fusion = (f32[128,64,128]{2,0,1:T(8,128)S(1)}, f32[128,64,128]{2,0,1:T(8,128)S(1)}) fusion(f32[128,64,128]{2,0,1:T(8,128)} %fusion.19, f32[128,64]{0,1:T(8,128)S(1)} %get-tuple-element.121, f32[128,64]{0,1:T(8,128)S(1)} %get-tuple-element.120, f32[128,64]{0,1:T(8,128)S(1)} %get-tuple-element.121, f32[128,64]{0,1:T(8,128)S(1)} %get-tuple-element.120, ...), kind=kOutput, calls=%fused_computation.7 | convolution fusion | flops 812646400 | bytes 13795328 | tf_op jit(solution)/shard_map/cond/branch_1_fun/kn,nmc->kmc/dot_general | solution.py:75
  154.0 6.4 %fusion.4 = f32[128,128,64]{1,2,0:T(8,128)S(1)} fusion(f32[128,64,128]{2,0,1:T(8,128)S(1)} %get-tuple-element.569, f32[64,64]{1,0:T(8,128)S(1)} %get-tuple-element.126), kind=kOutput, calls=%fused_computation.10 | convolution fusion | flops 805306368 | bytes 8404992 | tf_op jit(solution)/shard_map/cond/branch_1_fun/lm,kmc->klc/dot_general | solution.py:75
  160.4 7.1 %fusion.10 = f32[128,128,64]{1,2,0:T(8,128)S(1)} fusion(f32[128,128,64]{1,2,0:T(8,128)S(1)} %fusion.4, f32[128,64,128]{2,0,1:T(8,128)S(1)} %get-tuple-element.568, f32[64,64]{1,0:T(8,128)S(1)} %get-tuple-element.125), kind=kOutput, calls=%fused_computation.16 | convolution fusion | flops 806354944 | bytes 12599296 | tf_op jit(solution)/shard_map/cond/branch_1_fun/lm,kmc->klc/dot_general | solution.py:75
  167.5 6.6 %fusion.2 = f32[128,128,64]{1,2,0:T(8,128)S(1)} fusion(f32[128,64,128]{2,0,1:T(8,128)S(1)} %get-tuple-element.569, f32[64,64]{1,0:T(8,128)S(1)} %get-tuple-element.125), kind=kOutput, calls=%fused_computation.8 | convolution fusion | flops 805306368 | bytes 8404992 | tf_op jit(solution)/shard_map/cond/branch_1_fun/lm,kmc->klc/dot_general | solution.py:75
  174.1 11.3 %fusion.1 = (f32[128,64,128]{2,1,0:T(8,128)}, f32[128,64,128]{2,1,0:T(8,128)}) fusion(f32[128,64,128]{2,1,0:T(8,128)S(1)} %copy-done.2, f32[128,64,128]{2,1,0:T(8,128)S(1)} %copy-done.1, f32[128,128,64]{1,2,0:T(8,128)S(1)} %fusion.10, f32[128,128,64]{1,2,0:T(8,128)S(1)} %fusion.2, f32[64,64]{1,0:T(8,128)S(1)} %get-tuple-element.126, ...), kind=kOutput, calls=%fused_computation.3 | convolution fusion | flops 812646400 | bytes 29376512 | tf_op jit(solution)/shard_map/cond/branch_1_fun/lm,kmc->klc/dot_general | solution.py:75
  185.4 71.6 %conditional.5 = ((f32[128,64,128]{2,1,0:T(8,128)}, f32[128,64,128]{2,1,0:T(8,128)})) conditional(s32[]{:T(128)} %convert_element_type.244, (f32[128,64,128]{2,1,0:T(8,128)}, f32[128,64,128]{2,1,0:T(8,128)}) %conditional.4, (f32[128,128]{1,0:T(8,128)S(1)}, bf16[4096,128]{0,1:T(8,128)(2,1)}, f32[128,64]{0,1:T(8,128)S(1)}, f32[128,64]{0,1:T(8,128)S(1)}, ...), branch_computations={%region_2.3_spmd, %region_3.4_spmd} | conditional | flops 5253300224 | bytes 138346592 | solution.py:172
  191.1 5.4 %copy.163 = f32[128,64,128]{2,1,0:T(8,128)} copy(f32[128,64,128]{0,2,1:T(8,128)} %bitcast.342) | data formatting | bytes 8388608 | tf_op jit(solution)/shard_map/cond/branch_1_fun/reshape | solution.py:150
  199.7 5.4 %copy.159 = f32[128,64,128]{2,1,0:T(8,128)} copy(f32[128,64,128]{0,2,1:T(8,128)} %bitcast.343) | data formatting | bytes 8388608 | tf_op jit(solution)/shard_map/cond/branch_1_fun/reshape | solution.py:149
  206.8 3.9 fusion.56
  210.8 9.0 %multiply_add_fusion.4 = (f32[128,64,128]{2,0,1:T(8,128)S(1)}, f32[128,64,128]{2,0,1:T(8,128)S(1)}) fusion(f32[128,64,128]{2,0,1:T(8,128)} %fusion.56, f32[128,64]{0,1:T(8,128)S(1)} %get-tuple-element.172, f32[128,64]{0,1:T(8,128)S(1)} %get-tuple-element.171, f32[128,64]{0,1:T(8,128)S(1)} %get-tuple-element.172, f32[128,64]{0,1:T(8,128)S(1)} %get-tuple-element.171, ...), kind=kOutput, calls=%fused_computation.55 | convolution fusion | flops 812646400 | bytes 13795328 | tf_op jit(solution)/shard_map/cond/branch_1_fun/kn,nmc->kmc/dot_general | solution.py:75
  219.8 6.4 %fusion.41 = f32[128,128,64]{1,2,0:T(8,128)S(1)} fusion(f32[128,64,128]{2,0,1:T(8,128)S(1)} %get-tuple-element.573, f32[64,64]{1,0:T(8,128)S(1)} %get-tuple-element.177), kind=kOutput, calls=%fused_computation.58 | convolution fusion | flops 805306368 | bytes 8404992 | tf_op jit(solution)/shard_map/cond/branch_1_fun/lm,kmc->klc/dot_general | solution.py:75
  226.2 6.8 %fusion.47 = f32[128,128,64]{1,2,0:T(8,128)S(1)} fusion(f32[128,128,64]{1,2,0:T(8,128)S(1)} %fusion.41, f32[128,64,128]{2,0,1:T(8,128)S(1)} %get-tuple-element.572, f32[64,64]{1,0:T(8,128)S(1)} %get-tuple-element.176), kind=kOutput, calls=%fused_computation.64 | convolution fusion | flops 806354944 | bytes 12599296 | tf_op jit(solution)/shard_map/cond/branch_1_fun/lm,kmc->klc/dot_general | solution.py:75
  233.0 9.0 %fusion.39 = f32[128,128,64]{1,2,0:T(8,128)} fusion(f32[128,64,128]{2,0,1:T(8,128)S(1)} %get-tuple-element.573, f32[64,64]{1,0:T(8,128)S(1)} %get-tuple-element.176), kind=kOutput, calls=%fused_computation.56 | convolution fusion | flops 805306368 | bytes 8404992 | tf_op jit(solution)/shard_map/cond/branch_1_fun/lm,kmc->klc/dot_general | solution.py:75
  242.0 14.9 %fusion.36 = (f32[128,64,128]{2,1,0:T(8,128)}, f32[128,64,128]{2,1,0:T(8,128)}) fusion(f32[128,64,128]{2,1,0:T(8,128)} %copy.159, f32[128,64,128]{2,1,0:T(8,128)} %get-tuple-element.178, f32[128,64,128]{2,1,0:T(8,128)S(1)} %copy-done.4, f32[128,128,64]{1,2,0:T(8,128)S(1)} %fusion.47, f32[128,64,128]{2,1,0:T(8,128)} %get-tuple-element.127, ...), kind=kOutput, calls=%fused_computation.49 | convolution fusion | flops 814743552 | bytes 37765120 | tf_op jit(solution)/shard_map/cond/branch_1_fun/lm,kmc->klc/dot_general | solution.py:75
  257.1 71.8 %conditional.6 = ((f32[128,64,128]{2,1,0:T(8,128)}, f32[128,64,128]{2,1,0:T(8,128)})) conditional(s32[]{:T(128)} %convert_element_type.243, (f32[128,64,128]{2,1,0:T(8,128)}, f32[128,64,128]{2,1,0:T(8,128)}) %get-tuple-element.615, (f32[128,128]{1,0:T(8,128)S(1)}, bf16[4096,128]{0,1:T(8,128)(2,1)}, f32[128,64]{0,1:T(8,128)S(1)}, ...), branch_computations={%region_4.5_spmd, %region_5.6_spmd} | conditional | flops 5253300224 | bytes 138346592 | solution.py:172
  262.6 5.4 %copy.177 = f32[128,64,128]{2,1,0:T(8,128)} copy(f32[128,64,128]{0,2,1:T(8,128)} %bitcast.344) | data formatting | bytes 8388608 | tf_op jit(solution)/shard_map/cond/branch_1_fun/reshape | solution.py:150
  271.4 5.4 %copy.173 = f32[128,64,128]{2,1,0:T(8,128)} copy(f32[128,64,128]{0,2,1:T(8,128)} %bitcast.345) | data formatting | bytes 8388608 | tf_op jit(solution)/shard_map/cond/branch_1_fun/reshape | solution.py:149
  278.5 4.0 fusion.93
  282.6 9.0 %multiply_add_fusion.8 = (f32[128,64,128]{2,0,1:T(8,128)S(1)}, f32[128,64,128]{2,0,1:T(8,128)S(1)}) fusion(f32[128,64,128]{2,0,1:T(8,128)} %fusion.93, f32[128,64]{0,1:T(8,128)S(1)} %get-tuple-element.224, f32[128,64]{0,1:T(8,128)S(1)} %get-tuple-element.223, f32[128,64]{0,1:T(8,128)S(1)} %get-tuple-element.224, f32[128,64]{0,1:T(8,128)S(1)} %get-tuple-element.223, ...), kind=kOutput, calls=%fused_computation.103 | convolution fusion | flops 812646400 | bytes 13795328 | tf_op jit(solution)/shard_map/cond/branch_1_fun/kn,nmc->kmc/dot_general | solution.py:75
  291.5 6.4 %fusion.78 = f32[128,128,64]{1,2,0:T(8,128)S(1)} fusion(f32[128,64,128]{2,0,1:T(8,128)S(1)} %get-tuple-element.577, f32[64,64]{1,0:T(8,128)S(1)} %get-tuple-element.229), kind=kOutput, calls=%fused_computation.106 | convolution fusion | flops 805306368 | bytes 8404992 | tf_op jit(solution)/shard_map/cond/branch_1_fun/lm,kmc->klc/dot_general | solution.py:75
  297.9 6.8 %fusion.84 = f32[128,128,64]{1,2,0:T(8,128)S(1)} fusion(f32[128,128,64]{1,2,0:T(8,128)S(1)} %fusion.78, f32[128,64,128]{2,0,1:T(8,128)S(1)} %get-tuple-element.576, f32[64,64]{1,0:T(8,128)S(1)} %get-tuple-element.228), kind=kOutput, calls=%fused_computation.112 | convolution fusion | flops 806354944 | bytes 12599296 | tf_op jit(solution)/shard_map/cond/branch_1_fun/lm,kmc->klc/dot_general | solution.py:75
  304.8 9.0 %fusion.76 = f32[128,128,64]{1,2,0:T(8,128)} fusion(f32[128,64,128]{2,0,1:T(8,128)S(1)} %get-tuple-element.577, f32[64,64]{1,0:T(8,128)S(1)} %get-tuple-element.228), kind=kOutput, calls=%fused_computation.104 | convolution fusion | flops 805306368 | bytes 8404992 | tf_op jit(solution)/shard_map/cond/branch_1_fun/lm,kmc->klc/dot_general | solution.py:75
  313.7 14.9 %fusion.73 = (f32[128,64,128]{2,1,0:T(8,128)}, f32[128,64,128]{2,1,0:T(8,128)}) fusion(f32[128,64,128]{2,1,0:T(8,128)} %copy.173, f32[128,64,128]{2,1,0:T(8,128)} %get-tuple-element.230, f32[128,64,128]{2,1,0:T(8,128)S(1)} %copy-done.5, f32[128,128,64]{1,2,0:T(8,128)S(1)} %fusion.84, f32[128,64,128]{2,1,0:T(8,128)} %get-tuple-element.179, ...), kind=kOutput, calls=%fused_computation.97 | convolution fusion | flops 814743552 | bytes 37765120 | tf_op jit(solution)/shard_map/cond/branch_1_fun/lm,kmc->klc/dot_general | solution.py:75
  328.8 15.5 %conditional.7 = ((f32[128,64,128]{2,1,0:T(8,128)}, f32[128,64,128]{2,1,0:T(8,128)})) conditional(s32[]{:T(128)} %convert_element_type.242, (f32[128,64,128]{2,1,0:T(8,128)}, f32[128,64,128]{2,1,0:T(8,128)}) %get-tuple-element.616, (f32[128,128]{1,0:T(8,128)S(1)}, bf16[16384,128]{0,1:T(8,128)(2,1)}, f32[128,64]{0,1:T(8,128)S(1)}, ...), branch_computations={%region_6.7_spmd, %region_7.8_spmd} | conditional | flops 5253300224 | bytes 146735200 | solution.py:172
  344.3 5.8 %fusion.170 = f32[128,128,64]{1,2,0:T(8,128)S(1)} fusion(f32[128,64,128]{2,1,0:T(8,128)} %get-tuple-element.271), kind=kOutput, calls=%fused_computation.235 | convolution fusion | flops 805363712 | bytes 8388608 | tf_op jit(solution)/shard_map/lm,klc->kmc/dot_general | solution.py:75
  350.1 5.8 %fusion.172 = f32[128,128,64]{1,2,0:T(8,128)S(1)} fusion(f32[128,64,128]{2,1,0:T(8,128)} %get-tuple-element.270), kind=kOutput, calls=%fused_computation.237 | convolution fusion | flops 805363712 | bytes 8388608 | tf_op jit(solution)/shard_map/lm,klc->kmc/dot_general | solution.py:75
  355.9 5.8 %convolution_add_fusion.4 = f32[128,128,64]{1,2,0:T(8,128)S(1)} fusion(f32[128,128,64]{1,2,0:T(8,128)S(1)} %fusion.170, f32[128,64,128]{2,1,0:T(8,128)} %get-tuple-element.270), kind=kOutput, calls=%fused_computation.202 | convolution fusion | flops 806412288 | bytes 12582912 | tf_op jit(solution)/shard_map/lm,klc->kmc/dot_general | solution.py:75
  361.8 8.0 %subtract_bitcast_fusion = (f32[128,64,128]{2,1,0:T(8,128)S(1)}, f32[128,64,128]{2,1,0:T(8,128)S(1)}) fusion(f32[128,128,64]{1,2,0:T(8,128)S(1)} %convolution_add_fusion.4, f32[128,64]{1,0:T(8,128)S(1)} %copy.215, f32[128,64]{1,0:T(8,128)S(1)} %copy.212, f32[128,128,64]{1,2,0:T(8,128)S(1)} %fusion.172, f32[128,64,128]{2,1,0:T(8,128)} %get-tuple-element.271), kind=kOutput, calls=%fused_computation.200 | convolution fusion | flops 812703744 | bytes 21037056 | tf_op jit(solution)/shard_map/lm,klc->kmc/dot_general | solution.py:75
  369.8 4.7 fusion.148
  374.5 4.8 multiply_convert_fusion
  379.3 3.5 copy.218
  384.5 79.9 %all_to_all.63 = bf16[4096,4,32]{0,2,1:T(8,128)(2,1)S(1)} all-to-all(bf16[4096,4,32]{0,2,1:T(8,128)(2,1)S(1)} %convert_element_type.250), channel_id=1, replica_groups=mesh['ctx'=32,'fft'=4] {'fft'}, dimensions={1} | all-to-all | bytes 2097152 | tf_op jit(solution)/shard_map/all_to_all | solution.py:195
  466.6 25.0 %all_to_all.64 = bf16[32,512,32]{1,2,0:T(8,128)(2,1)S(1)} all-to-all(bf16[32,512,32]{1,2,0:T(8,128)(2,1)S(1)} %copy.220), channel_id=1, replica_groups=mesh['ctx'=32,'fft'=4] {'ctx'}, dimensions={0} | all-to-all | bytes 2097152 | tf_op jit(solution)/shard_map/all_to_all | solution.py:194
  491.6 3.4 fusion.153
  (83 shorter events, 43.4 us)
Async XLA Ops:
  6.5 109.4 %all-gather.2.cloned.1.call-start = ((), (), s32[]{:S(2)}) async-start(), calls=%async_computation.4 | async-start | bytes 5242880 | tf_op jit(solution)/shard_map/all_gather | solution.py:176
  7.4 10.3 %collective-permute-start = (bf16[2,3,1024]{2,0,1:T(2,128)(2,1)S(1)}, bf16[2,3,1024]{2,0,1:T(2,128)(2,1)S(1)}, u32[]{:S(2)}, u32[]{:S(2)}) collective-permute-start(bf16[2,3,1024]{2,0,1:T(2,128)(2,1)S(1)} %slice.86), channel_id=1, source_target_pairs={{0,4},{4,8},{8,12},{12,16},{16,20},{20,24},{24,28},{28,32},{32,36}... | collective-permute-start | bytes 36872 | tf_op jit(solution)/shard_map/ppermute | solution.py:14
  34.2 2.6 copy-start
  61.9 19.1 %copy-start.6 = (f32[4,1,2,16384]{3,2,1,0:T(2,128)S(1)}, f32[4,1,2,16384]{3,2,1,0:T(2,128)}, u32[]{:S(2)}) copy-start(f32[4,1,2,16384]{3,2,1,0:T(2,128)} %param.15) | copy-start | bytes 1572868
  167.5 6.6 %copy-start.1 = (f32[128,64,128]{2,1,0:T(8,128)S(1)}, f32[128,64,128]{2,1,0:T(8,128)}, u32[]{:S(2)}) copy-start(f32[128,64,128]{2,1,0:T(8,128)} %copy.149) | copy-start | bytes 12582916 | tf_op jit(solution)/shard_map/cond
  167.5 6.6 %copy-start.2 = (f32[128,64,128]{2,1,0:T(8,128)S(1)}, f32[128,64,128]{2,1,0:T(8,128)}, u32[]{:S(2)}) copy-start(f32[128,64,128]{2,1,0:T(8,128)} %copy.145) | copy-start | bytes 12582916 | tf_op jit(solution)/shard_map/cond
  233.0 9.0 %copy-start.4 = (f32[128,64,128]{2,1,0:T(8,128)S(1)}, f32[128,64,128]{2,1,0:T(8,128)}, u32[]{:S(2)}) copy-start(f32[128,64,128]{2,1,0:T(8,128)} %copy.163) | copy-start | bytes 12582916 | tf_op jit(solution)/shard_map/cond
  304.8 9.0 %copy-start.5 = (f32[128,64,128]{2,1,0:T(8,128)S(1)}, f32[128,64,128]{2,1,0:T(8,128)}, u32[]{:S(2)}) copy-start(f32[128,64,128]{2,1,0:T(8,128)} %copy.177) | copy-start | bytes 12582916 | tf_op jit(solution)/shard_map/cond
  464.4 27.2 %copy-start.7 = (f32[1024]{0:T(1024)S(1)}, f32[1024]{0:T(1024)}, u32[]{:S(2)}) copy-start(f32[1024]{0:T(1024)} %param.14) | copy-start | bytes 12292
Sparse Core Ops, SparseCore 0:
  81.2 34.7 all-gather.1
where the time goes:
time: 512 us; the launch traced here: 503 us
  matrix products  190 us (37%)
  blocking collectives  147 us (29%)
  local copies, waits for them, and re-layouts  84.4 us (16%)
  waiting for transfers between devices  34.8 us (7%)
  loops' own time  16.4 us (3%)
  between operations  13.9 us (3%)
  other arithmetic  13.5 us (3%)
    dot_general x42, matrix products, contract(): return jnp.einsum(form, table, data, precision=lax.Precision.HIGHEST)  190 us
    all_to_all x1, blocking collectives, local(): lax.all_to_all(long_rows.astype(jnp.bfloat16), 'fft', split_axis=1, conca...  79.9 us
    all_gather x1, waiting for transfers between devices, local(): lax.all_gather(part, 'fft', axis=0, tiled=True)  33.7 us
    all_to_all x1, blocking collectives, local(): lax.all_to_all(lax.all_to_all(long_rows.astype(jnp.bfloat16), 'fft', spli...  25 us
    all_to_all x1, blocking collectives, local(): lax.all_to_all(gated, 'ctx', split_axis=1, concat_axis=0, tiled=True)  24.1 us
    all_to_all x1, blocking collectives, local(): lax.all_to_all(lax.all_to_all(gated, 'ctx', split_axis=1, concat_axis=0,...  17.7 us
    another operation x4, loops' own time, add_block(): return lax.cond(lag_block >= 0, compute_sum, keep_sum, carry)  16.4 us
    reshape x3, local copies, waits for them, and re-layouts, filter_spectrum(): seg_im = jnp.repeat(jnp.moveaxis(seg_im, 0, -1), GROUP, axis=-1)  16.2 us
  transfers between devices with their start and end apart: 2, of which 2 were waited for; matrix products, arithmetic and copies ran while one was open for 1% of the time, Pallas kernels for 0%

commit v1 on v0

v1 whole, which is shorter than its diff:
```python
import functools

import jax
import jax.numpy as jnp
from jax import lax
from jax.experimental import pallas as pl
from jax.experimental.pallas import tpu as pltpu
from jax.sharding import PartitionSpec as P

GROUP = 16
LANES = 256
SUB = 256


def depthwise(rows_ref, halo, taps, scratch):
    rows = rows_ref.shape[0]
    scratch[8:, :] = rows_ref[...].astype(jnp.float32)
    scratch[8 - halo.shape[0] : 8, :] = halo
    total = taps[0:1, :] * scratch[8 : 8 + rows, :]
    for offset in range(1, taps.shape[0]):
        total = total + taps[offset : offset + 1, :] * scratch[8 - offset : 8 - offset + rows, :]
    return total


def gate_kernel(streams_ref, halo_ref, taps_ref, gated_ref, turned_ref, first, second):
    taps = taps_ref[...].astype(jnp.float32)
    halo = halo_ref[...].astype(jnp.float32)
    feat_one = depthwise(streams_ref.at[0], halo[1], taps[1], first)
    feat_two = depthwise(streams_ref.at[1], halo[2], taps[2], second)
    gated = (feat_one * feat_two).astype(jnp.bfloat16)
    gated_ref[...] = gated
    turned_ref[...] = gated.T


def finish_kernel(stream_ref, halo_ref, taps_ref, skip_ref, gated_ref, back_ref, out_ref, scratch):
    taps = taps_ref[0].astype(jnp.float32)
    query = depthwise(stream_ref.at[0], halo_ref[0].astype(jnp.float32), taps, scratch)
    inner = back_ref[...].T.astype(jnp.float32) + skip_ref[...] * gated_ref[...].astype(jnp.float32)
    out_ref[...] = (query * inner).astype(jnp.bfloat16)


def conv_kernel(signal_ref, taps_ref, out_ref, table, total):
    chunks, group, width = signal_ref.shape
    span = taps_ref.shape[-1]
    step = 1024
    for start in range(0, span - SUB, step):
        size = min(step, span - SUB - start)
        window = jnp.broadcast_to(taps_ref[0, :, start : start + size + SUB], (SUB, size + SUB))
        turned = pltpu.roll(window, 0, axis=1, stride=1, stride_axis=0)
        table[:, start : start + size] = turned[:, SUB:].astype(jnp.bfloat16)
    signal = signal_ref[...].reshape(chunks * group, width)
    for lag in range(chunks):
        rows = (chunks - lag) * group
        at = lag * width + SUB
        weights = jnp.concatenate(
            [table[:, at - half * SUB : at - half * SUB + width] for half in range(width // SUB)],
            axis=0,
        )
        part = jnp.dot(signal[:rows], weights, preferred_element_type=jnp.float32)
        if lag == 0:
            total[...] = part
        else:
            total[lag * group :, :] += part
    out_ref[...] = total[...].astype(jnp.bfloat16).reshape(chunks, group, width)


def local(qkv, short_w, skip, long_h):
    rows, _, channels = qkv.shape
    k_short = short_w.shape[0]
    n_ctx = lax.axis_size("ctx")
    chan = channels // n_ctx
    groups = chan // GROUP
    steps = channels // LANES
    streams = jnp.transpose(qkv, (1, 0, 2))
    weights = jnp.transpose(short_w, (1, 0, 2))
    halo = lax.ppermute(
        streams[:, rows - (k_short - 1) :, :], "ctx", [(s, s + 1) for s in range(n_ctx - 1)]
    )
    halo_spec = pl.BlockSpec((3, k_short - 1, LANES), lambda i: (0, 0, i))
    taps_spec = pl.BlockSpec((3, k_short, LANES), lambda i: (0, 0, i))
    token_spec = pl.BlockSpec((rows, LANES), lambda i: (0, i))
    turned_spec = pl.BlockSpec((LANES, rows), lambda i: (i, 0))
    gated, turned = pl.pallas_call(
        gate_kernel,
        grid=(steps,),
        in_specs=[
            pl.BlockSpec((pl.Element(2), pl.Element(rows), pl.Element(LANES)), lambda i: (1, 0, i * LANES)),
            halo_spec,
            taps_spec,
        ],
        out_specs=[token_spec, turned_spec],
        out_shape=[
            jax.ShapeDtypeStruct((rows, channels), jnp.bfloat16),
            jax.ShapeDtypeStruct((channels, rows), jnp.bfloat16),
        ],
        scratch_shapes=[pltpu.VMEM((rows + 8, LANES), jnp.float32)] * 2,
        name="gate",
    )(streams, halo, weights)
    columns = lax.all_to_all(turned.reshape(n_ctx, chan, rows), "ctx", 0, 0, tiled=True)
    own = lax.dynamic_index_in_dim(long_h, lax.axis_index("fft"), 0, False)
    taps = jnp.pad(own.reshape(groups, 1, -1), ((0, 0), (0, 0), (2 * SUB, 0)))
    span = taps.shape[-1]
    longconv = pl.pallas_call(
        conv_kernel,
        grid=(groups,),
        in_specs=[
            pl.BlockSpec((n_ctx, GROUP, rows), lambda g: (0, g, 0)),
            pl.BlockSpec((1, 1, span), lambda g: (g, 0, 0)),
        ],
        out_specs=pl.BlockSpec((n_ctx, GROUP, rows), lambda g: (0, g, 0)),
        out_shape=jax.ShapeDtypeStruct((n_ctx, chan, rows), jnp.bfloat16),
        scratch_shapes=[
            pltpu.VMEM((SUB, span - SUB), jnp.bfloat16),
            pltpu.VMEM((n_ctx * GROUP, rows), jnp.float32),
        ],
        name="longconv",
    )(columns, taps)
    back = lax.all_to_all(longconv, "ctx", 0, 0, tiled=True).reshape(channels, rows)
    return pl.pallas_call(
        finish_kernel,
        grid=(steps,),
        in_specs=[
            pl.BlockSpec((1, rows, LANES), lambda i: (0, 0, i)),
            halo_spec,
            taps_spec,
            pl.BlockSpec((1, LANES), lambda i: (0, i)),
            token_spec,
            turned_spec,
        ],
        out_specs=token_spec,
        out_shape=jax.ShapeDtypeStruct((rows, channels), jnp.bfloat16),
        scratch_shapes=[pltpu.VMEM((rows + 8, LANES), jnp.float32)],
        name="finish",
    )(streams, halo, weights, skip.reshape(1, channels), gated, back)


def solution(mesh):
    in_specs = (P("ctx", None, "fft"), P(None, None, "fft"), P("fft"), P(None, "ctx", None, None))
    out_specs = P("ctx", "fft")
    return jax.shard_map(local, mesh=mesh, in_specs=in_specs, out_specs=out_specs, check_vma=False)
```

time: 512 us -> 73.9 us (0.14); the launches traced: 503 us -> 73.3 us
  matrix products: 190 us -> 0 us
  blocking collectives: 147 us -> 19.3 us
  local copies, waits for them, and re-layouts: 84.4 us -> 4.66 us
  Pallas kernels: 0 us -> 21 us
  loops' own time: 16.4 us -> 0 us
  waiting for transfers between devices: 34.8 us -> 19.7 us
  between operations: 13.9 us -> 0.05 us
  other arithmetic: 13.5 us -> 0 us
    dot_general x42 -> x0, matrix products: 190 us -> none  [contract(): return jnp.einsum(form, table, data, precision=lax.Precision.HIGHEST)]
    all_to_all x4 -> x1, blocking collectives: 147 us -> 19.3 us  [local(): lax.all_to_all(longconv, 'ctx', 0, 0, tiled=True).reshape(channels, rows)]
    all_gather x1 -> x0, waiting for transfers between devices: 33.7 us -> none  [local(): lax.all_gather(part, 'fft', axis=0, tiled=True)]
    reshape x10 -> x1, local copies, waits for them, and re-layouts: 33.4 us -> 0.09 us  [local(): taps = jnp.pad(own.reshape(groups, 1, -1), ((0, 0), (0, 0), (2 * SUB, 0)))]
    pallas_call x0 -> x3, Pallas kernels: none -> 21 us  [the longest x1 12.1 us: local(): pl.pallas_call(conv_kernel, grid=(groups,), in_specs=[pl.BlockSpec((n_ctx...]
    another operation x4 -> x0, loops' own time: 16.4 us -> none  [add_block(): return lax.cond(lag_block >= 0, compute_sum, keep_sum, carry)]
    all_to_all x0 -> x1, waiting for transfers between devices: none -> 14.5 us  [local(): lax.all_to_all(turned.reshape(n_ctx, chan, rows), 'ctx', 0, 0, tiled=True)]
    broadcast_in_dim x6 -> x0, local copies, waits for them, and re-layouts: 13.9 us -> none  [the longest x3 7.04 us: filter_spectrum(): seg_re = jnp.repeat(jnp.moveaxis(seg_re, 0, -1), GROUP, axis=-1)]
  transfers between devices with their start and end apart: 2 -> 2, of which waited for: 2 -> 2; matrix products, arithmetic and copies ran while one was open for 1% -> 3% of each run, Pallas kernels for 0% -> 0%
where the time goes in v1:
time: 73.9 us; the launch traced here: 73.3 us
  Pallas kernels  21 us (28%)
  waiting for transfers between devices  19.7 us (27%)
  blocking collectives  19.3 us (26%)
  starting transfers between devices  8.65 us (12%)
  local copies, waits for them, and re-layouts  4.66 us (6%)
    all_to_all x1, blocking collectives, local(): lax.all_to_all(longconv, 'ctx', 0, 0, tiled=True).reshape(channels, rows)  19.3 us
    all_to_all x1, waiting for transfers between devices, local(): lax.all_to_all(turned.reshape(n_ctx, chan, rows), 'ctx', 0, 0, tiled=True)  14.5 us
    pallas_call x1, Pallas kernels, local(): pl.pallas_call(conv_kernel, grid=(groups,), in_specs=[pl.BlockSpec((n_ctx...  12.1 us
    ppermute x1, waiting for transfers between devices, local(): lax.ppermute(streams[:, rows - (k_short - 1):, :], 'ctx', [(s, s + 1) for...  5.13 us
    all_to_all x1, starting transfers between devices, local(): lax.all_to_all(turned.reshape(n_ctx, chan, rows), 'ctx', 0, 0, tiled=True)  4.83 us
    pallas_call x1, Pallas kernels, local(): pl.pallas_call(gate_kernel, grid=(steps,), in_specs=[pl.BlockSpec((pl.Ele...  4.52 us
    pallas_call x1, Pallas kernels, local(): pl.pallas_call(finish_kernel, grid=(steps,), in_specs=[pl.BlockSpec((1, r...  4.36 us
    ppermute x1, starting transfers between devices, local(): lax.ppermute(streams[:, rows - (k_short - 1):, :], 'ctx', [(s, s + 1) for...  3.83 us
  transfers between devices with their start and end apart: 2, of which 2 were waited for; matrix products, arithmetic and copies ran while one was open for 3% of the time, Pallas kernels for 0%

profile of v1, /device:TPU:6, one launch (start us, length us, event | category | flops | bytes accessed | tf_op | source)
XLA Modules:
  0.0 73.3 jit_solution(6869697279926408639)
XLA Ops:
  0.0 0.0 copy-start
  0.0 0.9 %slice.4 = bf16[3,2,1024]{2,1,0:T(2,128)(2,1)S(1)} slice(bf16[3,512,1024]{2,1,0:T(8,128)(2,1)} %bitcast.7), slice={[0:3], [510:512], [0:1024]} | slice | bytes 24576 | tf_op jit(solution)/shard_map/slice | solution.py:77
  0.9 3.8 %collective-permute-start = (bf16[3,2,1024]{2,1,0:T(2,128)(2,1)S(1)}, bf16[3,2,1024]{2,1,0:T(2,128)(2,1)S(1)}, u32[]{:S(2)}, u32[]{:S(2)}) collective-permute-start(bf16[3,2,1024]{2,1,0:T(2,128)(2,1)S(1)} %slice.4), channel_id=1, source_target_pairs={{0,4},{4,8},{8,12},{12,16},{16,20},{20,24},{24,28},{28,32},{32,36}... | collective-permute-start | bytes 36872 | tf_op jit(solution)/shard_map/ppermute | solution.py:76
  4.7 1.4 %copy.7 = bf16[3,3,1024]{2,0,1:T(4,128)(2,1)} copy(bf16[3,3,1024]{2,1,0:T(4,128)(2,1)} %param.5) | data formatting | bytes 36864 | tf_op args[1]
  6.1 5.1 %collective-permute-done.halo_ref = bf16[3,2,1024]{2,1,0:T(2,128)(2,1)S(1)} collective-permute-done((bf16[3,2,1024]{2,1,0:T(2,128)(2,1)S(1)}, bf16[3,2,1024]{2,1,0:T(2,128)(2,1)S(1)}, u32[]{:S(2)}, u32[]{:S(2)}) %collective-permute-start) | collective-permute-done | bytes 12320 | tf_op jit(solution)/shard_map/ppermute | solution.py:76
  11.2 0.0 copy-start.2
  11.2 0.6 copy-done.2
  11.8 4.5 %gate.1 = (bf16[512,1024]{1,0:T(8,128)(2,1)}, bf16[1024,512]{1,0:T(8,128)(2,1)}) custom-call(bf16[3,512,1024]{2,1,0:T(8,128)(2,1)} %bitcast.8, bf16[3,2,1024]{2,1,0:T(2,128)(2,1)} %copy-done.2, bf16[3,3,1024]{2,1,0:T(4,128)(2,1)} %bitcast.12), custom_call_target="tpu_custom_call" | custom-call | tf_op jit(solution)/shard_map/gate/pallas_call | solution.py:83
  16.3 4.8 %all-to-all-start = ((bf16[32,32,512]{2,1,0:T(8,128)(2,1)}), bf16[32,32,512]{2,1,0:T(8,128)(2,1)S(1)}, u32[]{:S(2)}, u32[]{:S(2)}) async-start(bf16[32,32,512]{2,1,0:T(8,128)(2,1)} %bitcast.11), calls=%async_computation | async-start | bytes 2097152 | tf_op jit(solution)/shard_map/all_to_all | solution.py:99
  21.2 0.0 copy-done
  21.2 0.1 reshape.15
  21.3 0.8 %pad.4.taps_ref = f32[2,1,16896]{2,1,0:T(1,128)} pad(f32[2,1,16384]{2,1,0:T(1,128)S(1)} %reshape.15, f32[]{:T(128)} %constant.12.clone.1), padding=0_0x0_0x512_0 | pad | bytes 266244 | tf_op jit(solution)/shard_map/jit(_pad)/pad | solution.py:101
  22.0 14.5 %all-to-all-done.signal_ref = bf16[32,32,512]{2,1,0:T(8,128)(2,1)S(1)} async-done(((bf16[32,32,512]{2,1,0:T(8,128)(2,1)}), bf16[32,32,512]{2,1,0:T(8,128)(2,1)S(1)}, u32[]{:S(2)}, u32[]{:S(2)}) %all-to-all-start) | async-done | bytes 1048608 | tf_op jit(solution)/shard_map/all_to_all | solution.py:99
  36.6 0.0 copy-start.1
  36.6 1.0 %copy-done.1 = bf16[32,32,512]{2,1,0:T(8,128)(2,1)} copy-done((bf16[32,32,512]{2,1,0:T(8,128)(2,1)}, bf16[32,32,512]{2,1,0:T(8,128)(2,1)S(1)}, u32[]{:S(2)}) %copy-start.1) | copy-done | bytes 1048600
  37.6 12.1 %longconv.1 = bf16[32,32,512]{2,1,0:T(8,128)(2,1)} custom-call(bf16[32,32,512]{2,1,0:T(8,128)(2,1)} %copy-done.1, f32[2,1,16896]{2,1,0:T(1,128)} %pad.4.taps_ref), custom_call_target="tpu_custom_call" | custom-call | tf_op jit(solution)/shard_map/longconv/pallas_call | solution.py:103
  49.6 19.3 %all_to_all.10 = bf16[32,32,512]{2,1,0:T(8,128)(2,1)} all-to-all(bf16[32,32,512]{2,1,0:T(8,128)(2,1)} %longconv.1), channel_id=1, replica_groups=mesh['ctx'=32,'fft'=4] {'ctx'}, dimensions={0} | all-to-all | bytes 2097152 | tf_op jit(solution)/shard_map/all_to_all | solution.py:118
  68.9 4.4 %finish.1 = bf16[512,1024]{1,0:T(8,128)(2,1)} custom-call(bf16[3,512,1024]{2,1,0:T(8,128)(2,1)} %bitcast.9, bf16[3,2,1024]{2,1,0:T(2,128)(2,1)} %copy-done.2, bf16[3,3,1024]{2,1,0:T(4,128)(2,1)} %bitcast.13, f32[1,1024]{1,0:T(1,128)} %bitcast.14, bf16[512,1024]{1,0:T(8,128)(2,1)} %get-tuple-element.7.gated_ref, bf16[1024,512]{1,0:T(8,128)(2,1)} %bitcast.10), custom_call_target="tpu_custom_call" | custom-call | tf_op jit(solution)/shard_map/finish/pallas_call | solution.py:119
  (1 shorter events, 0.0 us)
Async XLA Ops:
  0.0 21.2 %copy-start = (f32[4,1,2,16384]{3,2,1,0:T(2,128)S(1)}, f32[4,1,2,16384]{3,2,1,0:T(2,128)}, u32[]{:S(2)}) copy-start(f32[4,1,2,16384]{3,2,1,0:T(2,128)} %param.7) | copy-start | bytes 1572868
  0.9 10.3 %collective-permute-start = (bf16[3,2,1024]{2,1,0:T(2,128)(2,1)S(1)}, bf16[3,2,1024]{2,1,0:T(2,128)(2,1)S(1)}, u32[]{:S(2)}, u32[]{:S(2)}) collective-permute-start(bf16[3,2,1024]{2,1,0:T(2,128)(2,1)S(1)} %slice.4), channel_id=1, source_target_pairs={{0,4},{4,8},{8,12},{12,16},{16,20},{20,24},{24,28},{28,32},{32,36}... | collective-permute-start | bytes 36872 | tf_op jit(solution)/shard_map/ppermute | solution.py:76
  11.2 0.6 copy-start.2
  16.3 20.3 %all-to-all-start = ((bf16[32,32,512]{2,1,0:T(8,128)(2,1)}), bf16[32,32,512]{2,1,0:T(8,128)(2,1)S(1)}, u32[]{:S(2)}, u32[]{:S(2)}) async-start(bf16[32,32,512]{2,1,0:T(8,128)(2,1)} %bitcast.11), calls=%async_computation | async-start | bytes 2097152 | tf_op jit(solution)/shard_map/all_to_all | solution.py:99
  36.6 1.0 %copy-start.1 = (bf16[32,32,512]{2,1,0:T(8,128)(2,1)}, bf16[32,32,512]{2,1,0:T(8,128)(2,1)S(1)}, u32[]{:S(2)}) copy-start(bf16[32,32,512]{2,1,0:T(8,128)(2,1)S(1)} %all-to-all-done.signal_ref) | copy-start | bytes 3145732

commit v2 on v1

v2 whole, which is shorter than its diff:
```python
import jax
import jax.numpy as jnp
from jax import lax
from jax.experimental import pallas as pl
from jax.experimental.pallas import tpu as pltpu
from jax.sharding import PartitionSpec as P

GROUP = 16
LANES = 256
TILE = 256
SUB = 128
MIB = 1 << 20


def depthwise(rows_ref, halo, taps, scratch):
    rows = rows_ref.shape[0]
    scratch[8:, :] = rows_ref[...].astype(jnp.float32)
    scratch[8 - halo.shape[0] : 8, :] = halo
    total = taps[0] * scratch[8 : 8 + rows, :]
    for offset in range(1, len(taps)):
        total = total + taps[offset] * scratch[8 - offset : 8 - offset + rows, :]
    return total


def stream_taps(taps_ref, stream):
    return [taps_ref[j, stream : stream + 1, :].astype(jnp.float32) for j in range(taps_ref.shape[0])]


def gate_of(keys_ref, values_ref, halo_ref, taps_ref, scratch):
    halo = halo_ref[...].astype(jnp.float32)
    feat_one = depthwise(keys_ref, halo[1], stream_taps(taps_ref, 1), scratch.at[0])
    feat_two = depthwise(values_ref, halo[2], stream_taps(taps_ref, 2), scratch.at[1])
    return (feat_one * feat_two).astype(jnp.bfloat16)


def gate_kernel(streams_ref, halo_ref, taps_ref, turned_ref, scratch):
    gated = gate_of(streams_ref.at[0], streams_ref.at[1], halo_ref, taps_ref, scratch)
    turned_ref[...] = gated.T


def prepare_kernel(streams_ref, halo_ref, taps_ref, gated_ref, scratch):
    at = pl.ds(pl.multiple_of(pl.program_id(0) * LANES, LANES), LANES)
    gated_ref[:, at] = gate_of(streams_ref.at[0], streams_ref.at[1], halo_ref, taps_ref, scratch)


def build(taps_ref, group, kind, table, start, size):
    window = jnp.broadcast_to(taps_ref[group, kind, :, start : start + size + SUB], (SUB, size + SUB))
    turned = pltpu.roll(window, 0, axis=1, stride=1, stride_axis=0)
    table[group, kind, :, start : start + size] = turned[:, SUB:].astype(jnp.bfloat16)


def conv_kernel(signal_ref, taps_ref, out_ref, table, summed, held):
    chunks, chan, width = signal_ref.shape
    groups = chan // GROUP
    columns = table.shape[-1]
    pad = 2 * TILE - SUB

    for g in range(groups):
        rows = slice(g * GROUP, (g + 1) * GROUP)
        even = signal_ref[:, rows, :TILE].astype(jnp.float32)
        odd = signal_ref[:, rows, TILE:].astype(jnp.float32)
        summed[g] = (even + odd).astype(jnp.bfloat16)

    def left(g, product, chunk):
        if product == 2:
            return summed[g, chunk]
        return signal_ref[chunk, g * GROUP : (g + 1) * GROUP, product * TILE : (product + 1) * TILE]

    def factor(g, product, lag):
        at = pad + lag * width + (TILE if product == 1 else 0)
        kind = 1 if product == 2 else 0
        return jnp.concatenate(
            [table[g, kind, :, at - k * SUB : at - k * SUB + TILE] for k in range(TILE // SUB)], axis=0
        )

    def body(*sums):
        def total(g, product, chunk):
            return sums[(g * 2 + product % 2) * chunks + chunk]

        order = [(product, lag) for product in (2, 1, 0) for lag in range(chunks)]
        done = [0, 0]

        def stage(step):
            product, lag = order[step]
            kind = 1 if product == 2 else 0
            while done[kind] < min(pad + lag * width + 2 * TILE, columns):
                size = min(width, columns - done[kind])
                for g in range(groups):
                    build(taps_ref, g, kind, table, done[kind], size)
                done[kind] += size
            for g in range(groups):
                pltpu.matmul_push_rhs(factor(g, product, lag), step % 2, g)

        stage(0)
        last = [None] * groups
        for step, (product, lag) in enumerate(order):
            if step + 1 < len(order):
                stage(step + 1)
            for chunk in range(lag, chunks):
                for g in range(groups):
                    pltpu.matmul_acc_lhs(
                        total(g, product, chunk),
                        left(g, product, chunk - lag),
                        step % 2 if chunk == lag else None,
                    )
            for g in range(groups):
                rows = slice(g * GROUP, (g + 1) * GROUP)
                part = pltpu.matmul_pop(total(g, product, lag))
                if product == 2:
                    held[g, 0, lag] = part
                elif product == 1:
                    held[g, 0, lag] = held[g, 0, lag] - part
                    held[g, 1, lag] = part
                else:
                    even = part if lag == 0 else part + held[g, 1, lag - 1]
                    out_ref[lag, rows, :TILE] = even.astype(jnp.bfloat16)
                    out_ref[lag, rows, TILE:] = (held[g, 0, lag] - part).astype(jnp.bfloat16)

    pl.run_scoped(
        body,
        *[pltpu.ACC(g)((GROUP, TILE), jnp.float32) for g in range(groups) for _ in range(2 * chunks)],
    )


def finish_kernel(stream_ref, halo_ref, taps_ref, skip_ref, gated_ref, back_ref, out_ref, scratch):
    at = pl.ds(pl.multiple_of(pl.program_id(0) * LANES, LANES), LANES)
    halo = halo_ref[0].astype(jnp.float32)
    query = depthwise(stream_ref.at[0], halo, stream_taps(taps_ref, 0), scratch.at[0])
    inner = back_ref[at, :].T.astype(jnp.float32) + skip_ref[...] * gated_ref[:, at].astype(jnp.float32)
    out_ref[...] = (query * inner).astype(jnp.bfloat16)


def local(qkv, short_w, skip, long_h):
    rows, _, channels = qkv.shape
    k_short = short_w.shape[0]
    n_ctx = lax.axis_size("ctx")
    chan = channels // n_ctx
    groups = chan // GROUP
    steps = channels // LANES
    span = long_h.shape[-1]
    streams = jnp.transpose(qkv, (1, 0, 2))
    held = pltpu.with_memory_space_constraint(streams, pltpu.HBM)
    weights = pltpu.with_memory_space_constraint(short_w, pltpu.HBM)
    small = pltpu.CompilerParams(vmem_limit_bytes=40 * MIB)
    halo = lax.ppermute(
        streams[:, rows - (k_short - 1) :, :], "ctx", [(s, s + 1) for s in range(n_ctx - 1)]
    )
    halo_spec = pl.BlockSpec((3, k_short - 1, LANES), lambda i: (0, 0, i))
    taps_spec = pl.BlockSpec((k_short, 3, LANES), lambda i: (0, 0, i))
    pair_spec = pl.BlockSpec((pl.Element(2), pl.Element(rows), pl.Element(LANES)), lambda i: (1, 0, i * LANES))
    token_spec = pl.BlockSpec((rows, LANES), lambda i: (0, i))
    turned_spec = pl.BlockSpec((LANES, rows), lambda i: (i, 0))
    scratch = pltpu.VMEM((2, rows + 8, LANES), jnp.float32)
    turned = pl.pallas_call(
        gate_kernel,
        grid=(steps,),
        in_specs=[
            pair_spec,
            halo_spec,
            taps_spec,
        ],
        out_specs=turned_spec,
        out_shape=jax.ShapeDtypeStruct((channels, rows), jnp.bfloat16),
        scratch_shapes=[scratch],
        compiler_params=small,
        name="gate",
    )(held, halo, weights)
    columns = lax.all_to_all(turned.reshape(n_ctx, chan, rows), "ctx", 0, 0, tiled=True)
    own = lax.dynamic_index_in_dim(long_h, lax.axis_index("fft"), 0, False).reshape(groups, 1, span)
    near = jnp.pad(own, ((0, 0), (0, 0), (2 * TILE, 0)))
    both = near + jnp.pad(near[:, :, TILE:], ((0, 0), (0, 0), (0, TILE)))
    taps = jnp.stack([near, both], axis=1)
    whole = pl.BlockSpec(memory_space=pltpu.VMEM)
    gated = pl.pallas_call(
        prepare_kernel,
        grid=(steps,),
        in_specs=[pair_spec, halo_spec, taps_spec],
        out_specs=whole,
        out_shape=pltpu.VMEM((rows, channels), jnp.bfloat16),
        scratch_shapes=[scratch],
        compiler_params=small,
        cost_estimate=pl.CostEstimate(flops=32 * rows * channels, bytes_accessed=8 * MIB, transcendentals=0),
        name="prepare",
    )(held, halo, weights)
    longconv = pl.pallas_call(
        conv_kernel,
        in_specs=[whole, whole],
        out_specs=whole,
        out_shape=jax.ShapeDtypeStruct((n_ctx, chan, rows), jnp.bfloat16),
        scratch_shapes=[
            pltpu.VMEM((groups, 2, SUB, span + 2 * TILE - SUB), jnp.bfloat16),
            pltpu.VMEM((groups, n_ctx, GROUP, TILE), jnp.bfloat16),
            pltpu.VMEM((groups, 2, n_ctx, GROUP, TILE), jnp.float32),
        ],
        compiler_params=small,
        name="longconv",
    )(columns, taps)
    back = lax.all_to_all(longconv, "ctx", 0, 0, tiled=True).reshape(channels, rows)
    return pl.pallas_call(
        finish_kernel,
        grid=(steps,),
        in_specs=[
            pl.BlockSpec((1, rows, LANES), lambda i: (0, 0, i)),
            halo_spec,
            taps_spec,
            pl.BlockSpec((1, LANES), lambda i: (0, i)),
            whole,
            whole,
        ],
        out_specs=token_spec,
        out_shape=jax.ShapeDtypeStruct((rows, channels), jnp.bfloat16),
        scratch_shapes=[scratch],
        compiler_params=small,
        name="finish",
    )(
        held,
        halo,
        weights,
        skip.reshape(1, channels),
        pltpu.with_memory_space_constraint(gated, pltpu.VMEM),
        back,
    )


def solution(mesh):
    in_specs = (P("ctx", None, "fft"), P(None, None, "fft"), P("fft"), P(None, "ctx", None, None))
    out_specs = P("ctx", "fft")
    return jax.shard_map(local, mesh=mesh, in_specs=in_specs, out_specs=out_specs, check_vma=False)
```

time: 73.9 us -> 69.5 us (0.940)
  blocking collectives: 19.3 us -> 0 us
  waiting for transfers between devices: 19.7 us -> 31.3 us
  starting transfers between devices: 8.65 us -> 13.7 us
  local copies, waits for them, and re-layouts: 4.66 us -> 1 us
  Pallas kernels: 21 us -> 22.5 us
    all_to_all x1 -> x0, blocking collectives: 19.3 us -> none  [local(): lax.all_to_all(longconv, 'ctx', 0, 0, tiled=True).reshape(channels, rows)]
    all_to_all x0 -> x1, waiting for transfers between devices: none -> 10 us  [local(): lax.all_to_all(longconv, 'ctx', 0, 0, tiled=True).reshape(channels, rows)]
    all_to_all x0 -> x1, starting transfers between devices: none -> 5.02 us  [local(): lax.all_to_all(longconv, 'ctx', 0, 0, tiled=True).reshape(channels, rows)]
    unnamed x7 -> x4, local copies, waits for them, and re-layouts: 2.93 us -> 0.01 us
    pallas_call x2 -> x3, Pallas kernels: 16.6 us -> 18.5 us  [the longest x1 9.87 us: local(): pl.pallas_call(conv_kernel, in_specs=[whole, whole], out_specs=whole, out...]
    ppermute x1, waiting for transfers between devices: 5.13 us -> 6.15 us  [local(): lax.ppermute(streams[:, rows - (k_short - 1):, :], 'ctx', [(s, s + 1) for...]
    pad x1 -> x0, local copies, waits for them, and re-layouts: 0.75 us -> none  [local(): taps = jnp.pad(own.reshape(groups, 1, -1), ((0, 0), (0, 0), (2 * SUB, 0)))]
  transfers between devices with their start and end apart: 2 -> 3, of which waited for: 2 -> 3; matrix products, arithmetic and copies ran while one was open for 3% -> 1% of each run, Pallas kernels for 0% -> 6%
where the time goes in v2:
time: 69.5 us; the launch traced here: 69 us
  waiting for transfers between devices  31.3 us (45%)
  Pallas kernels  22.5 us (32%)
  starting transfers between devices  13.7 us (20%)
  local copies, waits for them, and re-layouts  1 us (1%)
    all_to_all x1, waiting for transfers between devices, local(): lax.all_to_all(turned.reshape(n_ctx, chan, rows), 'ctx', 0, 0, tiled=True)  15.2 us
    all_to_all x1, waiting for transfers between devices, local(): lax.all_to_all(longconv, 'ctx', 0, 0, tiled=True).reshape(channels, rows)  10 us
    pallas_call x1, Pallas kernels, local(): pl.pallas_call(conv_kernel, in_specs=[whole, whole], out_specs=whole, out...  9.87 us
    ppermute x1, waiting for transfers between devices, local(): lax.ppermute(streams[:, rows - (k_short - 1):, :], 'ctx', [(s, s + 1) for...  6.15 us
    all_to_all x1, starting transfers between devices, local(): lax.all_to_all(longconv, 'ctx', 0, 0, tiled=True).reshape(channels, rows)  5.02 us
    all_to_all x1, starting transfers between devices, local(): lax.all_to_all(turned.reshape(n_ctx, chan, rows), 'ctx', 0, 0, tiled=True)  4.83 us
    pallas_call x1, Pallas kernels, local(): pl.pallas_call(gate_kernel, grid=(steps,), in_specs=[pair_spec, halo_spec...  4.42 us
    pallas_call x1, Pallas kernels, local(): pl.pallas_call(prepare_kernel, grid=(steps,), in_specs=[pair_spec, halo_s...  4.25 us
  transfers between devices with their start and end apart: 3, of which 3 were waited for; matrix products, arithmetic and copies ran while one was open for 1% of the time, Pallas kernels for 6%

profile of v2, /device:TPU:6, one launch (start us, length us, event | category | flops | bytes accessed | tf_op | source)
XLA Modules:
  0.0 69.0 jit_solution(13625902053408635843)
XLA Ops:
  0.0 0.0 copy-start
  0.0 0.9 %slice.8 = bf16[3,2,1024]{2,1,0:T(2,128)(2,1)S(1)} slice(bf16[3,512,1024]{2,1,0:T(8,128)(2,1)} %bitcast.12), slice={[0:3], [510:512], [0:1024]} | slice | bytes 24576 | tf_op jit(solution)/shard_map/slice | solution.py:146
  0.9 3.8 %collective-permute-start = (bf16[3,2,1024]{2,1,0:T(2,128)(2,1)S(1)}, bf16[3,2,1024]{2,1,0:T(2,128)(2,1)S(1)}, u32[]{:S(2)}, u32[]{:S(2)}) collective-permute-start(bf16[3,2,1024]{2,1,0:T(2,128)(2,1)S(1)} %slice.8), channel_id=1, source_target_pairs={{0,4},{4,8},{8,12},{12,16},{16,20},{20,24},{24,28},{28,32},{32,36}... | collective-permute-start | bytes 36872 | tf_op jit(solution)/shard_map/ppermute | solution.py:145
  4.7 0.0 copy-done
  4.7 0.1 reshape.15
  4.9 0.2 pad_bitcast_fusion
  5.1 6.1 %collective-permute-done.halo_ref = bf16[3,2,1024]{2,1,0:T(2,128)(2,1)S(1)} collective-permute-done((bf16[3,2,1024]{2,1,0:T(2,128)(2,1)S(1)}, bf16[3,2,1024]{2,1,0:T(2,128)(2,1)S(1)}, u32[]{:S(2)}, u32[]{:S(2)}) %collective-permute-start) | collective-permute-done | bytes 12320 | tf_op jit(solution)/shard_map/ppermute | solution.py:145
  11.2 4.4 %gate.1 = bf16[1024,512]{1,0:T(8,128)(2,1)} custom-call(bf16[3,512,1024]{2,1,0:T(8,128)(2,1)} %bitcast.13, bf16[3,2,1024]{2,1,0:T(2,128)(2,1)S(1)} %collective-permute-done.halo_ref, bf16[3,3,1024]{2,1,0:T(4,128)(2,1)} %taps_ref.5), custom_call_target="tpu_custom_call" | custom-call | tf_op jit(solution)/shard_map/gate/pallas_call | solution.py:154
  15.6 4.8 %all-to-all-start = ((bf16[32,32,512]{2,1,0:T(8,128)(2,1)}), bf16[32,32,512]{2,1,0:T(8,128)(2,1)S(1)}, u32[]{:S(2)}, u32[]{:S(2)}) async-start(bf16[32,32,512]{2,1,0:T(8,128)(2,1)} %bitcast.2), calls=%async_computation | async-start | bytes 2097152 | tf_op jit(solution)/shard_map/all_to_all | solution.py:168
  20.5 0.2 pad_maximum_fusion.taps_ref
  20.7 15.2 %all-to-all-done.signal_ref = bf16[32,32,512]{2,1,0:T(8,128)(2,1)S(1)} async-done(((bf16[32,32,512]{2,1,0:T(8,128)(2,1)}), bf16[32,32,512]{2,1,0:T(8,128)(2,1)S(1)}, u32[]{:S(2)}, u32[]{:S(2)}) %all-to-all-start) | async-done | bytes 1048608 | tf_op jit(solution)/shard_map/all_to_all | solution.py:168
  35.9 9.9 %longconv.1 = bf16[32,32,512]{2,1,0:T(8,128)(2,1)} custom-call(bf16[32,32,512]{2,1,0:T(8,128)(2,1)S(1)} %all-to-all-done.signal_ref, f32[2,2,1,16896]{3,2,1,0:T(1,128)S(1)} %pad_maximum_fusion.taps_ref), custom_call_target="tpu_custom_call" | custom-call | tf_op jit(solution)/shard_map/longconv/pallas_call | solution.py:185
  45.7 0.0 copy-start.1
  45.7 5.0 %all-to-all-start.1 = ((bf16[32,32,512]{2,1,0:T(8,128)(2,1)}), bf16[32,32,512]{2,1,0:T(8,128)(2,1)S(1)}, u32[]{:S(2)}, u32[]{:S(2)}) async-start(bf16[32,32,512]{2,1,0:T(8,128)(2,1)} %longconv.1), calls=%async_computation.1 | async-start | bytes 2097152 | tf_op jit(solution)/shard_map/all_to_all | solution.py:198
  50.8 4.2 %prepare.1.gated_ref = bf16[512,1024]{1,0:T(8,128)(2,1)S(1)} custom-call(bf16[3,512,1024]{2,1,0:T(8,128)(2,1)} %bitcast.14, bf16[3,2,1024]{2,1,0:T(2,128)(2,1)S(1)} %collective-permute-done.halo_ref, bf16[3,3,1024]{2,1,0:T(4,128)(2,1)} %taps_ref.5), custom_call_target="tpu_custom_call" | custom-call | flops 16777216 | bytes 8388608 | tf_op jit(solution)/shard_map/prepare/pallas_call | solution.py:174
  55.0 10.0 %all-to-all-done.1 = bf16[32,32,512]{2,1,0:T(8,128)(2,1)S(1)} async-done(((bf16[32,32,512]{2,1,0:T(8,128)(2,1)}), bf16[32,32,512]{2,1,0:T(8,128)(2,1)S(1)}, u32[]{:S(2)}, u32[]{:S(2)}) %all-to-all-start.1) | async-done | bytes 1048608 | tf_op jit(solution)/shard_map/all_to_all | solution.py:198
  65.1 0.0 copy-done.1
  65.1 3.9 %finish.1 = bf16[512,1024]{1,0:T(8,128)(2,1)} custom-call(bf16[3,512,1024]{2,1,0:T(8,128)(2,1)} %bitcast.15, bf16[3,2,1024]{2,1,0:T(2,128)(2,1)S(1)} %collective-permute-done.halo_ref, bf16[3,3,1024]{2,1,0:T(4,128)(2,1)} %taps_ref.5, f32[1,1024]{1,0:T(1,128)S(1)} %bitcast.11, bf16[512,1024]{1,0:T(8,128)(2,1)S(1)} %prepare.1.gated_ref, ...), custom_call_target="tpu_custom_call" | custom-call | tf_op jit(solution)/shard_map/finish/pallas_call | solution.py:199
  (2 shorter events, 0.0 us)
Async XLA Ops:
  0.0 4.7 %copy-start = (f32[4,1,2,16384]{3,2,1,0:T(2,128)S(1)}, f32[4,1,2,16384]{3,2,1,0:T(2,128)}, u32[]{:S(2)}) copy-start(f32[4,1,2,16384]{3,2,1,0:T(2,128)} %param.7) | copy-start | bytes 1572868
  0.9 10.3 %collective-permute-start = (bf16[3,2,1024]{2,1,0:T(2,128)(2,1)S(1)}, bf16[3,2,1024]{2,1,0:T(2,128)(2,1)S(1)}, u32[]{:S(2)}, u32[]{:S(2)}) collective-permute-start(bf16[3,2,1024]{2,1,0:T(2,128)(2,1)S(1)} %slice.8), channel_id=1, source_target_pairs={{0,4},{4,8},{8,12},{12,16},{16,20},{20,24},{24,28},{28,32},{32,36}... | collective-permute-start | bytes 36872 | tf_op jit(solution)/shard_map/ppermute | solution.py:145
  15.6 20.2 %all-to-all-start = ((bf16[32,32,512]{2,1,0:T(8,128)(2,1)}), bf16[32,32,512]{2,1,0:T(8,128)(2,1)S(1)}, u32[]{:S(2)}, u32[]{:S(2)}) async-start(bf16[32,32,512]{2,1,0:T(8,128)(2,1)} %bitcast.2), calls=%async_computation | async-start | bytes 2097152 | tf_op jit(solution)/shard_map/all_to_all | solution.py:168
  45.7 19.3 %copy-start.1 = (f32[1024]{0:T(1024)S(1)}, f32[1024]{0:T(1024)}, u32[]{:S(2)}) copy-start(f32[1024]{0:T(1024)} %param.6) | copy-start | bytes 12292
  45.7 19.3 %all-to-all-start.1 = ((bf16[32,32,512]{2,1,0:T(8,128)(2,1)}), bf16[32,32,512]{2,1,0:T(8,128)(2,1)S(1)}, u32[]{:S(2)}, u32[]{:S(2)}) async-start(bf16[32,32,512]{2,1,0:T(8,128)(2,1)} %longconv.1), calls=%async_computation.1 | async-start | bytes 2097152 | tf_op jit(solution)/shard_map/all_to_all | solution.py:198

commit v3 on v2

--- a/solution.py
+++ b/solution.py
@@ -6,9 +6,10 @@
 from jax.sharding import PartitionSpec as P
 
 GROUP = 16
-LANES = 256
+LANES = 512
 TILE = 256
-SUB = 128
+SUB = 256
+SEND = 4
 MIB = 1 << 20
 
 
@@ -33,14 +34,50 @@
     return (feat_one * feat_two).astype(jnp.bfloat16)
 
 
+def depthwise_split(rows_ref, halo, taps, scratch):
+    rows = rows_ref.shape[0]
+    scratch[8:, :] = rows_ref[...].astype(jnp.float32)
+    scratch[8 - halo.shape[0] : 8, :] = halo
+    views = [scratch[pl.ds(8 - j, rows // 2, stride=2), :] for j in range(-1, len(taps))]
+    return [sum(taps[j] * views[j + 1 - odd] for j in range(len(taps))) for odd in (0, 1)]
+
+
 def gate_kernel(streams_ref, halo_ref, taps_ref, turned_ref, scratch):
-    gated = gate_of(streams_ref.at[0], streams_ref.at[1], halo_ref, taps_ref, scratch)
-    turned_ref[...] = gated.T
-
-
-def prepare_kernel(streams_ref, halo_ref, taps_ref, gated_ref, scratch):
+    rows = streams_ref.shape[1]
+    halo = halo_ref[...].astype(jnp.float32)
+    for slab in range(LANES // 128):
+        at = slice(slab * 128, (slab + 1) * 128)
+        parts = [
+            depthwise_split(
+                streams_ref.at[k, :, at],
+                halo[k + 1, :, at],
+                [tap[:, at] for tap in stream_taps(taps_ref, k + 1)],
+                scratch.at[slab, k],
+            )
+            for k in range(2)
+        ]
+        for odd in (0, 1):
+            scratch[slab, 2, pl.ds(odd, rows // 2, stride=2), :] = parts[0][odd] * parts[1][odd]
+        turned_ref[at, :] = scratch[slab, 2, :rows, :].astype(jnp.bfloat16).T
+
+
+def prepare_kernel(streams_ref, halo_ref, taps_ref, query_ref, gated_ref, scratch):
     at = pl.ds(pl.multiple_of(pl.program_id(0) * LANES, LANES), LANES)
-    gated_ref[:, at] = gate_of(streams_ref.at[0], streams_ref.at[1], halo_ref, taps_ref, scratch)
+    halo = halo_ref[0].astype(jnp.float32)
+    query_ref[:, at] = depthwise(streams_ref.at[0], halo, stream_taps(taps_ref, 0), scratch.at[0])
+    gated_ref[...] = gate_of(streams_ref.at[1], streams_ref.at[2], halo_ref, taps_ref, scratch)
+
+
+def filter_kernel(own_ref, taps_ref, out_ref):
+    span = taps_ref.shape[-1]
+    for g in range(taps_ref.shape[1]):
+        taps = taps_ref[0, g : g + 1, :]
+        out_ref[g, 0, :, : 2 * TILE] = jnp.zeros((1, 2 * TILE), jnp.float32)
+        out_ref[g, 0, :, 2 * TILE :] = taps
+        out_ref[g, 1, :, :TILE] = jnp.zeros((1, TILE), jnp.float32)
+        out_ref[g, 1, :, TILE : 2 * TILE] = taps[:, :TILE]
+        out_ref[g, 1, :, 2 * TILE : span + TILE] = taps[:, : span - TILE] + taps[:, TILE:]
+        out_ref[g, 1, :, span + TILE :] = taps[:, span - TILE :]
 
 
 def build(taps_ref, group, kind, table, start, size):
@@ -49,7 +86,7 @@
     table[group, kind, :, start : start + size] = turned[:, SUB:].astype(jnp.bfloat16)
 
 
-def conv_kernel(signal_ref, taps_ref, out_ref, table, summed, held):
+def conv_kernel(signal_ref, taps_ref, out_hbm, table, summed, held, out_ref, sent):
     chunks, chan, width = signal_ref.shape
     groups = chan // GROUP
     columns = table.shape[-1]
@@ -72,6 +109,10 @@
         return jnp.concatenate(
             [table[g, kind, :, at - k * SUB : at - k * SUB + TILE] for k in range(TILE // SUB)], axis=0
         )
+
+    def send(piece):
+        at = pl.ds(piece * SEND, SEND)
+        return pltpu.make_async_copy(out_ref.at[at], out_hbm.at[at], sent.at[piece])
 
     def body(*sums):
         def total(g, product, chunk):
@@ -92,7 +133,6 @@
                 pltpu.matmul_push_rhs(factor(g, product, lag), step % 2, g)
 
         stage(0)
-        last = [None] * groups
         for step, (product, lag) in enumerate(order):
             if step + 1 < len(order):
                 stage(step + 1)
@@ -115,19 +155,21 @@
                     even = part if lag == 0 else part + held[g, 1, lag - 1]
                     out_ref[lag, rows, :TILE] = even.astype(jnp.bfloat16)
                     out_ref[lag, rows, TILE:] = (held[g, 0, lag] - part).astype(jnp.bfloat16)
+            if product == 0 and (lag + 1) % SEND == 0:
+                send(lag // SEND).start()
 
     pl.run_scoped(
         body,
         *[pltpu.ACC(g)((GROUP, TILE), jnp.float32) for g in range(groups) for _ in range(2 * chunks)],
     )
-
-
-def finish_kernel(stream_ref, halo_ref, taps_ref, skip_ref, gated_ref, back_ref, out_ref, scratch):
+    for piece in range(chunks // SEND):
+        send(piece).wait()
+
+
+def finish_kernel(query_ref, skip_ref, gated_ref, back_ref, out_ref):
     at = pl.ds(pl.multiple_of(pl.program_id(0) * LANES, LANES), LANES)
-    halo = halo_ref[0].astype(jnp.float32)
-    query = depthwise(stream_ref.at[0], halo, stream_taps(taps_ref, 0), scratch.at[0])
-    inner = back_ref[at, :].T.astype(jnp.float32) + skip_ref[...] * gated_ref[:, at].astype(jnp.float32)
-    out_ref[...] = (query * inner).astype(jnp.bfloat16)
+    inner = back_ref[at, :].T.astype(jnp.float32) + skip_ref[...] * gated_ref[...].astype(jnp.float32)
+    out_ref[...] = (query_ref[:, at] * inner).astype(jnp.bfloat16)
 
 
 def local(qkv, short_w, skip, long_h):
@@ -161,22 +203,32 @@
         ],
         out_specs=turned_spec,
         out_shape=jax.ShapeDtypeStruct((channels, rows), jnp.bfloat16),
-        scratch_shapes=[scratch],
+        scratch_shapes=[pltpu.VMEM((LANES // 128, 3, rows + 8, 128), jnp.float32)],
         compiler_params=small,
         name="gate",
     )(held, halo, weights)
     columns = lax.all_to_all(turned.reshape(n_ctx, chan, rows), "ctx", 0, 0, tiled=True)
-    own = lax.dynamic_index_in_dim(long_h, lax.axis_index("fft"), 0, False).reshape(groups, 1, span)
-    near = jnp.pad(own, ((0, 0), (0, 0), (2 * TILE, 0)))
-    both = near + jnp.pad(near[:, :, TILE:], ((0, 0), (0, 0), (0, TILE)))
-    taps = jnp.stack([near, both], axis=1)
+    filters = pltpu.with_memory_space_constraint(long_h.reshape(-1, groups, span), pltpu.HBM)
+    taps = pl.pallas_call(
+        filter_kernel,
+        grid_spec=pltpu.PrefetchScalarGridSpec(
+            num_scalar_prefetch=1,
+            grid=(1,),
+            in_specs=[pl.BlockSpec((1, groups, span), lambda i, own: (own[0], 0, 0))],
+            out_specs=pl.BlockSpec((groups, 2, 1, span + 2 * TILE), lambda i, own: (0, 0, 0, 0)),
+        ),
+        out_shape=jax.ShapeDtypeStruct((groups, 2, 1, span + 2 * TILE), jnp.float32),
+        compiler_params=small,
+        cost_estimate=pl.CostEstimate(flops=8 * span, bytes_accessed=2 * MIB, transcendentals=0),
+        name="filter",
+    )(lax.axis_index("fft").reshape(1), filters)
     whole = pl.BlockSpec(memory_space=pltpu.VMEM)
-    gated = pl.pallas_call(
+    query, gated = pl.pallas_call(
         prepare_kernel,
         grid=(steps,),
-        in_specs=[pair_spec, halo_spec, taps_spec],
-        out_specs=whole,
-        out_shape=pltpu.VMEM((rows, channels), jnp.bfloat16),
+        in_specs=[pl.BlockSpec((3, rows, LANES), lambda i: (0, 0, i)), halo_spec, taps_spec],
+        out_specs=[whole, token_spec],
+        out_shape=[pltpu.VMEM((rows, channels), jnp.float32), pltpu.HBM((rows, channels), jnp.bfloat16)],
         scratch_shapes=[scratch],
         compiler_params=small,
         cost_estimate=pl.CostEstimate(flops=32 * rows * channels, bytes_accessed=8 * MIB, transcendentals=0),
@@ -185,12 +237,14 @@
     longconv = pl.pallas_call(
         conv_kernel,
         in_specs=[whole, whole],
-        out_specs=whole,
-        out_shape=jax.ShapeDtypeStruct((n_ctx, chan, rows), jnp.bfloat16),
+        out_specs=pl.BlockSpec(memory_space=pltpu.HBM),
+        out_shape=pltpu.HBM((n_ctx, chan, rows), jnp.bfloat16),
         scratch_shapes=[
             pltpu.VMEM((groups, 2, SUB, span + 2 * TILE - SUB), jnp.bfloat16),
             pltpu.VMEM((groups, n_ctx, GROUP, TILE), jnp.bfloat16),
             pltpu.VMEM((groups, 2, n_ctx, GROUP, TILE), jnp.float32),
+            pltpu.VMEM((n_ctx, chan, rows), jnp.bfloat16),
+            pltpu.SemaphoreType.DMA((n_ctx // SEND,)),
         ],
         compiler_params=small,
         name="longconv",
@@ -199,25 +253,15 @@
     return pl.pallas_call(
         finish_kernel,
         grid=(steps,),
-        in_specs=[
-            pl.BlockSpec((1, rows, LANES), lambda i: (0, 0, i)),
-            halo_spec,
-            taps_spec,
-            pl.BlockSpec((1, LANES), lambda i: (0, i)),
-            whole,
-            whole,
-        ],
+        in_specs=[whole, pl.BlockSpec((1, LANES), lambda i: (0, i)), token_spec, whole],
         out_specs=token_spec,
         out_shape=jax.ShapeDtypeStruct((rows, channels), jnp.bfloat16),
-        scratch_shapes=[scratch],
         compiler_params=small,
         name="finish",
     )(
-        held,
-        halo,
-        weights,
+        pltpu.with_memory_space_constraint(query, pltpu.VMEM),
         skip.reshape(1, channels),
-        pltpu.with_memory_space_constraint(gated, pltpu.VMEM),
+        pltpu.with_memory_space_constraint(gated, pltpu.HBM),
         back,
     )
 

time: 69.5 us -> 66.6 us (0.958)
  waiting for transfers between devices: 31.3 us -> 29 us
    all_to_all x1, waiting for transfers between devices: 10 us -> 8.03 us  [local(): lax.all_to_all(longconv, 'ctx', 0, 0, tiled=True).reshape(channels, rows)]
    pallas_call x3 -> x4, Pallas kernels: 18.1 us -> 19.2 us  [the longest x1 9.61 us: local(): pl.pallas_call(conv_kernel, in_specs=[whole, whole], out_specs=pl.BlockSp...]
    pallas_call x1, Pallas kernels: 4.42 us -> 3.51 us  [local(): pl.pallas_call(gate_kernel, grid=(steps,), in_specs=[pair_spec, halo_spec...]
  transfers between devices with their start and end apart: 3 -> 3, of which waited for: 3 -> 3; matrix products, arithmetic and copies ran while one was open for 1% -> 0% of each run, Pallas kernels for 6% -> 11%
where the time goes in v3:
time: 66.6 us; the launch traced here: 66.1 us
  waiting for transfers between devices  29 us (44%)
  Pallas kernels  22.7 us (34%)
  starting transfers between devices  13.6 us (20%)
  local copies, waits for them, and re-layouts  0.82 us (1%)
    all_to_all x1, waiting for transfers between devices, local(): lax.all_to_all(turned.reshape(n_ctx, chan, rows), 'ctx', 0, 0, tiled=True)  14.5 us
    pallas_call x1, Pallas kernels, local(): pl.pallas_call(conv_kernel, in_specs=[whole, whole], out_specs=pl.BlockSp...  9.61 us
    all_to_all x1, waiting for transfers between devices, local(): lax.all_to_all(longconv, 'ctx', 0, 0, tiled=True).reshape(channels, rows)  8.03 us
    ppermute x1, waiting for transfers between devices, local(): lax.ppermute(streams[:, rows - (k_short - 1):, :], 'ctx', [(s, s + 1) for...  6.49 us
    pallas_call x1, Pallas kernels, local(): pl.pallas_call(prepare_kernel, grid=(steps,), in_specs=[pl.BlockSpec((3,...  6.25 us
    all_to_all x1, starting transfers between devices, local(): lax.all_to_all(longconv, 'ctx', 0, 0, tiled=True).reshape(channels, rows)  4.91 us
    all_to_all x1, starting transfers between devices, local(): lax.all_to_all(turned.reshape(n_ctx, chan, rows), 'ctx', 0, 0, tiled=True)  4.83 us
    ppermute x1, starting transfers between devices, local(): lax.ppermute(streams[:, rows - (k_short - 1):, :], 'ctx', [(s, s + 1) for...  3.83 us
  transfers between devices with their start and end apart: 3, of which 3 were waited for; matrix products, arithmetic and copies ran while one was open for 0% of the time, Pallas kernels for 11%

profile of v3, /device:TPU:6, one launch (start us, length us, event | category | flops | bytes accessed | tf_op | source)
XLA Modules:
  0.0 66.1 jit_solution(11088674530786888071)
XLA Ops:
  0.0 0.8 %slice.4 = bf16[3,2,1024]{2,1,0:T(2,128)(2,1)S(1)} slice(bf16[3,512,1024]{2,1,0:T(8,128)(2,1)} %bitcast.8), slice={[0:3], [510:512], [0:1024]} | slice | bytes 24576 | tf_op jit(solution)/shard_map/slice | solution.py:188
  0.8 3.8 %collective-permute-start = (bf16[3,2,1024]{2,1,0:T(2,128)(2,1)S(1)}, bf16[3,2,1024]{2,1,0:T(2,128)(2,1)S(1)}, u32[]{:S(2)}, u32[]{:S(2)}) collective-permute-start(bf16[3,2,1024]{2,1,0:T(2,128)(2,1)S(1)} %slice.4), channel_id=1, source_target_pairs={{0,4},{4,8},{8,12},{12,16},{16,20},{20,24},{24,28},{28,32},{32,36}... | collective-permute-start | bytes 36872 | tf_op jit(solution)/shard_map/ppermute | solution.py:187
  4.7 6.5 %collective-permute-done.halo_ref = bf16[3,2,1024]{2,1,0:T(2,128)(2,1)S(1)} collective-permute-done((bf16[3,2,1024]{2,1,0:T(2,128)(2,1)S(1)}, bf16[3,2,1024]{2,1,0:T(2,128)(2,1)S(1)}, u32[]{:S(2)}, u32[]{:S(2)}) %collective-permute-start) | collective-permute-done | bytes 12320 | tf_op jit(solution)/shard_map/ppermute | solution.py:187
  11.1 3.5 %gate.1 = bf16[1024,512]{1,0:T(8,128)(2,1)} custom-call(bf16[3,512,1024]{2,1,0:T(8,128)(2,1)} %bitcast.9, bf16[3,2,1024]{2,1,0:T(2,128)(2,1)S(1)} %collective-permute-done.halo_ref, bf16[3,3,1024]{2,1,0:T(4,128)(2,1)} %taps_ref.3), custom_call_target="tpu_custom_call" | custom-call | tf_op jit(solution)/shard_map/gate/pallas_call | solution.py:196
  14.7 4.8 %all-to-all-start = ((bf16[32,32,512]{2,1,0:T(8,128)(2,1)}), bf16[32,32,512]{2,1,0:T(8,128)(2,1)S(1)}, u32[]{:S(2)}, u32[]{:S(2)}) async-start(bf16[32,32,512]{2,1,0:T(8,128)(2,1)} %bitcast.2), calls=%async_computation | async-start | bytes 2097152 | tf_op jit(solution)/shard_map/all_to_all | solution.py:210
  19.5 0.9 %filter.1.taps_ref = f32[2,2,1,16896]{3,2,1,0:T(1,128)S(1)} custom-call(s32[1]{0:T(128)} %bitcast.3.own_ref, f32[4,2,16384]{2,1,0:T(2,128)} %bitcast.11), custom_call_target="tpu_custom_call" | custom-call | flops 131072 | bytes 2097152 | tf_op jit(solution)/shard_map/filter/pallas_call | solution.py:212
  20.4 14.5 %all-to-all-done.signal_ref = bf16[32,32,512]{2,1,0:T(8,128)(2,1)S(1)} async-done(((bf16[32,32,512]{2,1,0:T(8,128)(2,1)}), bf16[32,32,512]{2,1,0:T(8,128)(2,1)S(1)}, u32[]{:S(2)}, u32[]{:S(2)}) %all-to-all-start) | async-done | bytes 1048608 | tf_op jit(solution)/shard_map/all_to_all | solution.py:210
  34.9 9.6 %longconv.1 = bf16[32,32,512]{2,1,0:T(8,128)(2,1)} custom-call(bf16[32,32,512]{2,1,0:T(8,128)(2,1)S(1)} %all-to-all-done.signal_ref, f32[2,2,1,16896]{3,2,1,0:T(1,128)S(1)} %filter.1.taps_ref), custom_call_target="tpu_custom_call" | custom-call | tf_op jit(solution)/shard_map/longconv/pallas_call | solution.py:237
  44.5 0.0 copy-start
  44.5 4.9 %all-to-all-start.1 = ((bf16[32,32,512]{2,1,0:T(8,128)(2,1)}), bf16[32,32,512]{2,1,0:T(8,128)(2,1)S(1)}, u32[]{:S(2)}, u32[]{:S(2)}) async-start(bf16[32,32,512]{2,1,0:T(8,128)(2,1)} %longconv.1), calls=%async_computation.1 | async-start | bytes 2097152 | tf_op jit(solution)/shard_map/all_to_all | solution.py:252
  49.4 6.3 %prepare.1 = (f32[512,1024]{1,0:T(8,128)S(1)}, bf16[512,1024]{1,0:T(8,128)(2,1)}) custom-call(bf16[3,512,1024]{2,1,0:T(8,128)(2,1)} %bitcast.10, bf16[3,2,1024]{2,1,0:T(2,128)(2,1)S(1)} %collective-permute-done.halo_ref, bf16[3,3,1024]{2,1,0:T(4,128)(2,1)} %taps_ref.3), custom_call_target="tpu_custom_call" | custom-call | flops 16777216 | bytes 8388608 | tf_op jit(solution)/shard_map/prepare/pallas_call | solution.py:226
  55.7 8.0 %all-to-all-done.1 = bf16[32,32,512]{2,1,0:T(8,128)(2,1)S(1)} async-done(((bf16[32,32,512]{2,1,0:T(8,128)(2,1)}), bf16[32,32,512]{2,1,0:T(8,128)(2,1)S(1)}, u32[]{:S(2)}, u32[]{:S(2)}) %all-to-all-start.1) | async-done | bytes 1048608 | tf_op jit(solution)/shard_map/all_to_all | solution.py:252
  63.7 0.0 copy-done
  63.7 2.4 %finish.1 = bf16[512,1024]{1,0:T(8,128)(2,1)} custom-call(f32[512,1024]{1,0:T(8,128)S(1)} %get-tuple-element.7.query_ref, f32[1,1024]{1,0:T(1,128)S(1)} %bitcast.7, bf16[512,1024]{1,0:T(8,128)(2,1)} %get-tuple-element.8.gated_ref, bf16[1024,512]{1,0:T(8,128)(2,1)S(1)} %bitcast.6), custom_call_target="tpu_custom_call" | custom-call | tf_op jit(solution)/shard_map/finish/pallas_call | solution.py:253
Async XLA Ops:
  0.8 10.3 %collective-permute-start = (bf16[3,2,1024]{2,1,0:T(2,128)(2,1)S(1)}, bf16[3,2,1024]{2,1,0:T(2,128)(2,1)S(1)}, u32[]{:S(2)}, u32[]{:S(2)}) collective-permute-start(bf16[3,2,1024]{2,1,0:T(2,128)(2,1)S(1)} %slice.4), channel_id=1, source_target_pairs={{0,4},{4,8},{8,12},{12,16},{16,20},{20,24},{24,28},{28,32},{32,36}... | collective-permute-start | bytes 36872 | tf_op jit(solution)/shard_map/ppermute | solution.py:187
  14.7 20.2 %all-to-all-start = ((bf16[32,32,512]{2,1,0:T(8,128)(2,1)}), bf16[32,32,512]{2,1,0:T(8,128)(2,1)S(1)}, u32[]{:S(2)}, u32[]{:S(2)}) async-start(bf16[32,32,512]{2,1,0:T(8,128)(2,1)} %bitcast.2), calls=%async_computation | async-start | bytes 2097152 | tf_op jit(solution)/shard_map/all_to_all | solution.py:210
  44.5 19.2 %copy-start = (f32[1024]{0:T(1024)S(1)}, f32[1024]{0:T(1024)}, u32[]{:S(2)}) copy-start(f32[1024]{0:T(1024)} %param.6) | copy-start | bytes 12292
  44.5 19.2 %all-to-all-start.1 = ((bf16[32,32,512]{2,1,0:T(8,128)(2,1)}), bf16[32,32,512]{2,1,0:T(8,128)(2,1)S(1)}, u32[]{:S(2)}, u32[]{:S(2)}) async-start(bf16[32,32,512]{2,1,0:T(8,128)(2,1)} %longconv.1), calls=%async_computation.1 | async-start | bytes 2097152 | tf_op jit(solution)/shard_map/all_to_all | solution.py:252

commit v4 on v3

--- a/solution.py
+++ b/solution.py
@@ -8,7 +8,9 @@
 GROUP = 16
 LANES = 512
 TILE = 256
-SUB = 256
+SUB = 128
+SPREAD = 4
+DELAY = 2
 SEND = 4
 MIB = 1 << 20
 
@@ -125,24 +127,14 @@
             product, lag = order[step]
             kind = 1 if product == 2 else 0
             while done[kind] < min(pad + lag * width + 2 * TILE, columns):
-                size = min(width, columns - done[kind])
+                size = min(SPREAD * width if done[kind] else width, columns - done[kind])
                 for g in range(groups):
                     build(taps_ref, g, kind, table, done[kind], size)
                 done[kind] += size
             for g in range(groups):
                 pltpu.matmul_push_rhs(factor(g, product, lag), step % 2, g)
 
-        stage(0)
-        for step, (product, lag) in enumerate(order):
-            if step + 1 < len(order):
-                stage(step + 1)
-            for chunk in range(lag, chunks):
-                for g in range(groups):
-                    pltpu.matmul_acc_lhs(
-                        total(g, product, chunk),
-                        left(g, product, chunk - lag),
-                        step % 2 if chunk == lag else None,
-                    )
+        def finish(product, lag):
             for g in range(groups):
                 rows = slice(g * GROUP, (g + 1) * GROUP)
                 part = pltpu.matmul_pop(total(g, product, lag))
@@ -157,6 +149,22 @@
                     out_ref[lag, rows, TILE:] = (held[g, 0, lag] - part).astype(jnp.bfloat16)
             if product == 0 and (lag + 1) % SEND == 0:
                 send(lag // SEND).start()
+
+        stage(0)
+        for step, (product, lag) in enumerate(order):
+            if step + 1 < len(order):
+                stage(step + 1)
+            for chunk in range(lag, chunks):
+                for g in range(groups):
+                    pltpu.matmul_acc_lhs(
+                        total(g, product, chunk),
+                        left(g, product, chunk - lag),
+                        step % 2 if chunk == lag else None,
+                    )
+            if step >= DELAY:
+                finish(*order[step - DELAY])
+        for step in range(len(order) - DELAY, len(order)):
+            finish(*order[step])
 
     pl.run_scoped(
         body,

time: 66.6 us -> 65.8 us (0.988)
  Pallas kernels: 22.7 us -> 22 us
    pallas_call x1, Pallas kernels: 9.61 us -> 8.9 us  [local(): pl.pallas_call(conv_kernel, in_specs=[whole, whole], out_specs=pl.BlockSp...]
where the time goes in v4:
time: 65.8 us; the launch traced here: 65.4 us
  waiting for transfers between devices  29 us (44%)
  Pallas kernels  22 us (33%)
  starting transfers between devices  13.6 us (21%)
  local copies, waits for them, and re-layouts  0.82 us (1%)
    all_to_all x1, waiting for transfers between devices, local(): lax.all_to_all(turned.reshape(n_ctx, chan, rows), 'ctx', 0, 0, tiled=True)  14.5 us
    pallas_call x1, Pallas kernels, local(): pl.pallas_call(conv_kernel, in_specs=[whole, whole], out_specs=pl.BlockSp...  8.9 us
    all_to_all x1, waiting for transfers between devices, local(): lax.all_to_all(longconv, 'ctx', 0, 0, tiled=True).reshape(channels, rows)  8.03 us
    ppermute x1, waiting for transfers between devices, local(): lax.ppermute(streams[:, rows - (k_short - 1):, :], 'ctx', [(s, s + 1) for...  6.49 us
    pallas_call x1, Pallas kernels, local(): pl.pallas_call(prepare_kernel, grid=(steps,), in_specs=[pl.BlockSpec((3,...  6.25 us
    all_to_all x1, starting transfers between devices, local(): lax.all_to_all(longconv, 'ctx', 0, 0, tiled=True).reshape(channels, rows)  4.9 us
    all_to_all x1, starting transfers between devices, local(): lax.all_to_all(turned.reshape(n_ctx, chan, rows), 'ctx', 0, 0, tiled=True)  4.83 us
    ppermute x1, starting transfers between devices, local(): lax.ppermute(streams[:, rows - (k_short - 1):, :], 'ctx', [(s, s + 1) for...  3.83 us
  transfers between devices with their start and end apart: 3, of which 3 were waited for; matrix products, arithmetic and copies ran while one was open for 0% of the time, Pallas kernels for 11%

profile of v4, /device:TPU:6, one launch (start us, length us, event | category | flops | bytes accessed | tf_op | source)
XLA Modules:
  0.0 65.4 jit_solution(4210517140277130557)
XLA Ops:
  0.0 0.8 %slice.4 = bf16[3,2,1024]{2,1,0:T(2,128)(2,1)S(1)} slice(bf16[3,512,1024]{2,1,0:T(8,128)(2,1)} %bitcast.8), slice={[0:3], [510:512], [0:1024]} | slice | bytes 24576 | tf_op jit(solution)/shard_map/slice | solution.py:196
  0.8 3.8 %collective-permute-start = (bf16[3,2,1024]{2,1,0:T(2,128)(2,1)S(1)}, bf16[3,2,1024]{2,1,0:T(2,128)(2,1)S(1)}, u32[]{:S(2)}, u32[]{:S(2)}) collective-permute-start(bf16[3,2,1024]{2,1,0:T(2,128)(2,1)S(1)} %slice.4), channel_id=1, source_target_pairs={{0,4},{4,8},{8,12},{12,16},{16,20},{20,24},{24,28},{28,32},{32,36}... | collective-permute-start | bytes 36872 | tf_op jit(solution)/shard_map/ppermute | solution.py:195
  4.7 6.5 %collective-permute-done.halo_ref = bf16[3,2,1024]{2,1,0:T(2,128)(2,1)S(1)} collective-permute-done((bf16[3,2,1024]{2,1,0:T(2,128)(2,1)S(1)}, bf16[3,2,1024]{2,1,0:T(2,128)(2,1)S(1)}, u32[]{:S(2)}, u32[]{:S(2)}) %collective-permute-start) | collective-permute-done | bytes 12320 | tf_op jit(solution)/shard_map/ppermute | solution.py:195
  11.1 3.5 %gate.1 = bf16[1024,512]{1,0:T(8,128)(2,1)} custom-call(bf16[3,512,1024]{2,1,0:T(8,128)(2,1)} %bitcast.9, bf16[3,2,1024]{2,1,0:T(2,128)(2,1)S(1)} %collective-permute-done.halo_ref, bf16[3,3,1024]{2,1,0:T(4,128)(2,1)} %taps_ref.3), custom_call_target="tpu_custom_call" | custom-call | tf_op jit(solution)/shard_map/gate/pallas_call | solution.py:204
  14.7 4.8 %all-to-all-start = ((bf16[32,32,512]{2,1,0:T(8,128)(2,1)}), bf16[32,32,512]{2,1,0:T(8,128)(2,1)S(1)}, u32[]{:S(2)}, u32[]{:S(2)}) async-start(bf16[32,32,512]{2,1,0:T(8,128)(2,1)} %bitcast.2), calls=%async_computation | async-start | bytes 2097152 | tf_op jit(solution)/shard_map/all_to_all | solution.py:218
  19.5 0.9 %filter.1.taps_ref = f32[2,2,1,16896]{3,2,1,0:T(1,128)S(1)} custom-call(s32[1]{0:T(128)} %bitcast.3.own_ref, f32[4,2,16384]{2,1,0:T(2,128)} %bitcast.11), custom_call_target="tpu_custom_call" | custom-call | flops 131072 | bytes 2097152 | tf_op jit(solution)/shard_map/filter/pallas_call | solution.py:220
  20.4 14.5 %all-to-all-done.signal_ref = bf16[32,32,512]{2,1,0:T(8,128)(2,1)S(1)} async-done(((bf16[32,32,512]{2,1,0:T(8,128)(2,1)}), bf16[32,32,512]{2,1,0:T(8,128)(2,1)S(1)}, u32[]{:S(2)}, u32[]{:S(2)}) %all-to-all-start) | async-done | bytes 1048608 | tf_op jit(solution)/shard_map/all_to_all | solution.py:218
  34.9 8.9 %longconv.1 = bf16[32,32,512]{2,1,0:T(8,128)(2,1)} custom-call(bf16[32,32,512]{2,1,0:T(8,128)(2,1)S(1)} %all-to-all-done.signal_ref, f32[2,2,1,16896]{3,2,1,0:T(1,128)S(1)} %filter.1.taps_ref), custom_call_target="tpu_custom_call" | custom-call | tf_op jit(solution)/shard_map/longconv/pallas_call | solution.py:245
  43.8 0.0 copy-start
  43.8 4.9 %all-to-all-start.1 = ((bf16[32,32,512]{2,1,0:T(8,128)(2,1)}), bf16[32,32,512]{2,1,0:T(8,128)(2,1)S(1)}, u32[]{:S(2)}, u32[]{:S(2)}) async-start(bf16[32,32,512]{2,1,0:T(8,128)(2,1)} %longconv.1), calls=%async_computation.1 | async-start | bytes 2097152 | tf_op jit(solution)/shard_map/all_to_all | solution.py:260
  48.7 6.3 %prepare.1 = (f32[512,1024]{1,0:T(8,128)S(1)}, bf16[512,1024]{1,0:T(8,128)(2,1)}) custom-call(bf16[3,512,1024]{2,1,0:T(8,128)(2,1)} %bitcast.10, bf16[3,2,1024]{2,1,0:T(2,128)(2,1)S(1)} %collective-permute-done.halo_ref, bf16[3,3,1024]{2,1,0:T(4,128)(2,1)} %taps_ref.3), custom_call_target="tpu_custom_call" | custom-call | flops 16777216 | bytes 8388608 | tf_op jit(solution)/shard_map/prepare/pallas_call | solution.py:234
  55.0 8.0 %all-to-all-done.1 = bf16[32,32,512]{2,1,0:T(8,128)(2,1)S(1)} async-done(((bf16[32,32,512]{2,1,0:T(8,128)(2,1)}), bf16[32,32,512]{2,1,0:T(8,128)(2,1)S(1)}, u32[]{:S(2)}, u32[]{:S(2)}) %all-to-all-start.1) | async-done | bytes 1048608 | tf_op jit(solution)/shard_map/all_to_all | solution.py:260
  63.0 0.0 copy-done
  63.0 2.4 %finish.1 = bf16[512,1024]{1,0:T(8,128)(2,1)} custom-call(f32[512,1024]{1,0:T(8,128)S(1)} %get-tuple-element.7.query_ref, f32[1,1024]{1,0:T(1,128)S(1)} %bitcast.7, bf16[512,1024]{1,0:T(8,128)(2,1)} %get-tuple-element.8.gated_ref, bf16[1024,512]{1,0:T(8,128)(2,1)S(1)} %bitcast.6), custom_call_target="tpu_custom_call" | custom-call | tf_op jit(solution)/shard_map/finish/pallas_call | solution.py:261
Async XLA Ops:
  0.8 10.3 %collective-permute-start = (bf16[3,2,1024]{2,1,0:T(2,128)(2,1)S(1)}, bf16[3,2,1024]{2,1,0:T(2,128)(2,1)S(1)}, u32[]{:S(2)}, u32[]{:S(2)}) collective-permute-start(bf16[3,2,1024]{2,1,0:T(2,128)(2,1)S(1)} %slice.4), channel_id=1, source_target_pairs={{0,4},{4,8},{8,12},{12,16},{16,20},{20,24},{24,28},{28,32},{32,36}... | collective-permute-start | bytes 36872 | tf_op jit(solution)/shard_map/ppermute | solution.py:195
  14.7 20.2 %all-to-all-start = ((bf16[32,32,512]{2,1,0:T(8,128)(2,1)}), bf16[32,32,512]{2,1,0:T(8,128)(2,1)S(1)}, u32[]{:S(2)}, u32[]{:S(2)}) async-start(bf16[32,32,512]{2,1,0:T(8,128)(2,1)} %bitcast.2), calls=%async_computation | async-start | bytes 2097152 | tf_op jit(solution)/shard_map/all_to_all | solution.py:218
  43.8 19.2 %copy-start = (f32[1024]{0:T(1024)S(1)}, f32[1024]{0:T(1024)}, u32[]{:S(2)}) copy-start(f32[1024]{0:T(1024)} %param.6) | copy-start | bytes 12292
  43.8 19.2 %all-to-all-start.1 = ((bf16[32,32,512]{2,1,0:T(8,128)(2,1)}), bf16[32,32,512]{2,1,0:T(8,128)(2,1)S(1)}, u32[]{:S(2)}, u32[]{:S(2)}) async-start(bf16[32,32,512]{2,1,0:T(8,128)(2,1)} %longconv.1), calls=%async_computation.1 | async-start | bytes 2097152 | tf_op jit(solution)/shard_map/all_to_all | solution.py:260
